TPU v7x, 256 devices: a whole 4x4x8 slice. The times are simulated.
256 devices in a mesh: leaf: 32 (over z, x), rank: 4 (over y), rhs: 2 (over core).
Axes of the slice: x: 4, y: 4, z: 8, core: 2. Of those that a mesh axis runs over, the one named last changes fastest.
Arguments:
- rhs: float32 [65536, 512], P(('leaf', 'rank'), 'rhs'), parts along dimension 1, may hold values from -40 to 40
- order: int32 [65536], P(('leaf', 'rank')), may hold values from 0 to 65535, as said below
- diag: float32 [65536], P(('leaf', 'rank')), may hold values from 2 to 8
- blocks: bfloat16 [1536, 128, 128], P(('leaf', 'rank')), may hold values from -0.3125 to 0.3125
- near_rows: int32 [1536], P(('leaf', 'rank')), may hold values from 0 to 511, as said below
- near_cols: int32 [1536], P(('leaf', 'rank')), may hold values from 0 to 511, as said below
- gen_u: bfloat16 [5, 65536, 128], P(None, 'leaf', 'rank'), may hold values from -0.5 to 0.5
- gen_v: bfloat16 [5, 65536, 128], P(None, 'leaf', 'rank'), may hold values from -0.03125 to 0.03125
Outputs:
- solution: float32 [65536, 512], P(('leaf', 'rank'), 'rhs'), parts along dimension 1
- residual: float32 [65536, 512], P(('leaf', 'rank'), 'rhs'), parts along dimension 1
There are 2 independent parts, one for each index of `rhs`. A program takes and returns all parts, laid end to end along the dimension named above; an argument that names none is the same for every part. Nothing has to cross between parts.
Inputs may be any that keep to these rules, and one draw needn't show every extreme that they name: `order`: each aligned run of 512 entries is a permutation of the panel numbers of that run. `near_rows`: block k's row is one of the 4 block rows of the device that holds block k; every block row is named, at least once by a block whose column equals it. `near_cols`: block k's column lies in the same subtree of 2048 panels as its row, at most 4 block columns away from it.
All inputs are finite; a program needn't handle non-finite values.
Results may differ from a plain program's by a relative error of at most 0.0035.
Values may be sent and summed in bfloat16 or wider, within the bound.
A program may use at most 64 MiB of HBM per device.

v0:
```python
import jax
import jax.numpy as jnp
from jax import lax
from jax.sharding import PartitionSpec as P

EPSILON = 1e-06


def from_partner(value, axis, apart):
    mask = 2**apart
    pairs = [(source, source ^ mask) for source in range(lax.axis_size(axis))]
    return lax.ppermute(value, axis, pairs)


def local(rhs, order, diag, blocks, near_rows, near_cols, gen_u, gen_v):
    panel_count, columns_count = rhs.shape
    levels = gen_v.shape[0]
    leaf_panels = gen_v.shape[1]
    block_size = blocks.shape[1]
    rows_dev = panel_count // block_size
    rows_leaf = leaf_panels // block_size
    device = lax.axis_index(("leaf", "rank"))
    leaf_id = lax.axis_index("leaf")
    local_order = order - device * panel_count
    local_rows = near_rows - device * rows_dev
    local_cols = near_cols - leaf_id * rows_leaf
    selector = (jnp.arange(rows_dev, dtype=jnp.int32)[:, None] == local_rows[None, :]).astype(
        jnp.float32
    )

    def tree_sums(coeffs):
        partial_value = [coeffs[level] for level in range(levels)]
        sibling = []
        for level in range(levels):
            stacked = jnp.stack(partial_value[level:], 0)
            received = from_partner(stacked, "leaf", level)
            sibling.append(received[0])
            for upper in range(level + 1, levels):
                partial_value[upper] = partial_value[upper] + received[upper - level]
        return jnp.stack(sibling, 0)

    def apply(vector):
        narrow = vector.astype(jnp.bfloat16)
        subtree = lax.all_gather(narrow, "rank", axis=0, tiled=True)
        coeffs = jnp.einsum("lpk,pn->lkn", gen_v, subtree, preferred_element_type=jnp.float32)
        column_blocks = subtree.reshape(rows_leaf, block_size, columns_count)[local_cols]
        sibling = tree_sums(coeffs).astype(jnp.bfloat16)
        products = jnp.einsum(
            "kij,kjn->kin", blocks, column_blocks, preferred_element_type=jnp.float32
        )
        near = jnp.einsum(
            "rk,kin->rin", selector, products, precision=lax.Precision.HIGHEST
        ).reshape(panel_count, columns_count)
        far = lax.psum_scatter(
            jnp.einsum("lpk,lkn->pn", gen_u, sibling, preferred_element_type=jnp.float32),
            "rank",
            scatter_dimension=0,
            tiled=True,
        )
        return diag[:, None] * vector + near + far

    start = rhs[local_order]
    beta = jnp.sqrt(lax.psum(jnp.sum(start * start, axis=0), ("leaf", "rank")) + EPSILON)
    basis_one = start / beta
    image_one = apply(basis_one)
    h11 = lax.psum(jnp.sum(basis_one * image_one, axis=0), ("leaf", "rank"))
    rest_one = image_one - h11 * basis_one
    h21 = jnp.sqrt(lax.psum(jnp.sum(rest_one * rest_one, axis=0), ("leaf", "rank")) + EPSILON)
    basis_two = rest_one / h21
    image_two = apply(basis_two)
    h12, h22 = lax.psum(
        (jnp.sum(basis_one * image_two, axis=0), jnp.sum(basis_two * image_two, axis=0)),
        ("leaf", "rank"),
    )
    rest_two = image_two - h12 * basis_one - h22 * basis_two
    h32 = jnp.sqrt(lax.psum(jnp.sum(rest_two * rest_two, axis=0), ("leaf", "rank")) + EPSILON)
    r_one = jnp.sqrt(h11 * h11 + h21 * h21)
    cos_one = h11 / r_one
    sin_one = h21 / r_one
    top = cos_one * h12 + sin_one * h22
    low = cos_one * h22 - sin_one * h12
    r_two = jnp.sqrt(low * low + h32 * h32)
    y_two = low / r_two * (-sin_one * beta) / r_two
    y_one = (cos_one * beta - top * y_two) / r_one
    tree_solution = y_one * basis_one + y_two * basis_two
    tree_residual = (
        (beta - y_one * h11 - y_two * h12) * basis_one
        - (y_one * h21 + y_two * h22) * basis_two
        - y_two * rest_two
    )
    solution = jnp.zeros_like(rhs).at[local_order].set(tree_solution)
    residual = jnp.zeros_like(rhs).at[local_order].set(tree_residual)
    return (solution, residual)


def solution(mesh):
    in_specs = (
        P(("leaf", "rank"), "rhs"),
        P(("leaf", "rank")),
        P(("leaf", "rank")),
        P(("leaf", "rank"), None, None),
        P(("leaf", "rank")),
        P(("leaf", "rank")),
        P(None, "leaf", "rank"),
        P(None, "leaf", "rank"),
    )
    out_specs = (P(("leaf", "rank"), "rhs"), P(("leaf", "rank"), "rhs"))
    return jax.shard_map(local, mesh=mesh, in_specs=in_specs, out_specs=out_specs, check_vma=False)
```

profile of v0, /device:TPU:8, one launch (start us, length us, event | category | flops | bytes accessed | tf_op | source)
XLA Modules:
  0.0 1938.2 jit_solution(10514694611025003767)
XLA Ops:
  8.0 2.7 gather_fusion
  10.8 346.4 %psum.42 = f32[256]{0:T(256)S(1)} all-reduce(f32[256]{0:T(256)S(1)} %multiply_reduce_fusion.5), channel_id=1, replica_groups=mesh['leaf'=32,'rank'=4,'rhs'=2] {'leaf','rank'}, use_global_device_ids=true, to_apply=%region_1.0 | all-reduce | flops 256 | bytes 2048 | tf_op jit(solution)/shard_map/psum | solution.py:63
  357.1 0.8 fusion.33
  357.9 23.9 %all-gather.3.cloned.1.call-done = bf16[2048,256]{1,0:T(8,128)(2,1)} async-done(((bf16[512,256]{1,0:T(8,128)(2,1)}), bf16[2048,256]{1,0:T(8,128)(2,1)}) %all-gather.3.cloned.1.call-update) | async-done | bytes 1048592 | tf_op jit(solution)/shard_map/all_gather | solution.py:44
  381.9 1.6 fusion.37
  383.4 1.6 collective-permute-start
  385.0 3.9 collective-permute-done
  388.9 3.1 collective-permute-start.1
  391.9 3.5 collective-permute-done.1
  395.5 1.6 collective-permute-start.2
  397.1 3.8 collective-permute-done.2
  400.9 1.9 collective-permute-start.3
  402.8 3.3 collective-permute-done.3
  406.2 6.2 collective-permute-start.4
  412.4 1.7 collective-permute-done.4
  414.2 1.9 convolution_bitcast_fusion.1
  417.1 1.6 fusion.35
  418.6 2.2 copy.17
  420.8 0.8 fusion.2
  421.8 27.5 %reduce-scatter.3.cloned.1.call-done = f32[512,256]{1,0:T(8,128)} async-done(((f32[2048,256]{1,0:T(8,128)}), f32[512,256]{1,0:T(8,128)}) %reduce-scatter.3.cloned.1.call-update) | async-done | bytes 524304 | tf_op jit(solution)/shard_map/reduce_scatter | solution.py:54
  449.3 1.2 multiply_reduce_fusion.4
  450.5 344.0 %psum.43 = f32[256]{0:T(256)S(1)} all-reduce(f32[256]{0:T(256)S(1)} %multiply_reduce_fusion.4), channel_id=1, replica_groups=mesh['leaf'=32,'rank'=4,'rhs'=2] {'leaf','rank'}, use_global_device_ids=true, to_apply=%region_4.0 | all-reduce | flops 256 | bytes 2048 | tf_op jit(solution)/shard_map/psum | solution.py:66
  794.5 1.2 multiply_reduce_fusion.3
  795.7 347.8 %psum.44 = f32[256]{0:T(256)S(1)} all-reduce(f32[256]{0:T(256)S(1)} %get-tuple-element.10), channel_id=1, replica_groups=mesh['leaf'=32,'rank'=4,'rhs'=2] {'leaf','rank'}, use_global_device_ids=true, to_apply=%region_6.0 | all-reduce | flops 256 | bytes 2048 | tf_op jit(solution)/shard_map/psum | solution.py:68
  1143.5 0.8 fusion.32
  1144.4 20.1 %all-gather.5.cloned.1.call-done = bf16[2048,256]{1,0:T(8,128)(2,1)} async-done(((bf16[512,256]{1,0:T(8,128)(2,1)}), bf16[2048,256]{1,0:T(8,128)(2,1)}) %all-gather.5.cloned.1.call-update) | async-done | bytes 1048592 | tf_op jit(solution)/shard_map/all_gather | solution.py:44
  1164.5 1.6 fusion.38
  1166.0 1.6 collective-permute-start.5
  1167.6 3.9 collective-permute-done.5
  1171.5 3.1 collective-permute-start.6
  1174.6 3.5 collective-permute-done.6
  1178.1 1.6 collective-permute-start.7
  1179.7 3.8 collective-permute-done.7
  1183.5 1.9 collective-permute-start.8
  1185.4 3.3 collective-permute-done.8
  1188.8 6.4 collective-permute-start.9
  1195.2 1.7 collective-permute-done.9
  1196.9 1.9 convolution_bitcast_fusion
  1198.9 1.5 gather_fusion.2
  1200.4 1.6 fusion.36
  1202.1 1.9 copy.19
  1204.0 2.4 fusion
  1206.5 25.5 %reduce-scatter.5.cloned.1.call-done = f32[512,256]{1,0:T(8,128)} async-done(((f32[2048,256]{1,0:T(8,128)}), f32[512,256]{1,0:T(8,128)}) %reduce-scatter.5.cloned.1.call-update) | async-done | bytes 524304 | tf_op jit(solution)/shard_map/reduce_scatter | solution.py:54
  1232.1 1.3 multiply_reduce_fusion.2
  1233.3 344.0 %all-reduce = (f32[256]{0:T(256)S(1)}, f32[256]{0:T(256)S(1)}) all-reduce(f32[256]{0:T(256)S(1)} %get-tuple-element.3, f32[256]{0:T(256)S(1)} %get-tuple-element.2), channel_id=1, replica_groups=mesh['leaf'=32,'rank'=4,'rhs'=2] {'leaf','rank'}, use_global_device_ids=true, to_apply=%region_11.0 | all-reduce | flops 512 | bytes 4096 | tf_op jit(solution)/shard_map/psum | solution.py:71
  1577.5 347.8 %psum.47 = f32[256]{0:T(256)S(1)} all-reduce(f32[256]{0:T(256)S(1)} %multiply_reduce_fusion), channel_id=1, replica_groups=mesh['leaf'=32,'rank'=4,'rhs'=2] {'leaf','rank'}, use_global_device_ids=true, to_apply=%region_13.0 | all-reduce | flops 256 | bytes 2048 | tf_op jit(solution)/shard_map/psum | solution.py:76
  1925.3 3.1 scatter_custom_fusion
  1928.4 3.2 scatter_custom_fusion.1
  (62 shorter events, 2.6 us)
Async XLA Ops:
  7.2 407.0 %copy-start = (bf16[5,2048,32]{1,2,0:T(8,128)(2,1)S(1)}, bf16[5,2048,32]{1,2,0:T(8,128)(2,1)}, u32[]{:S(2)}) copy-start(bf16[5,2048,32]{1,2,0:T(8,128)(2,1)} %param.14) | copy-start | bytes 1966084
  7.2 374.7 %all-gather.3.cloned.1.call-start = ((), (), s32[]{:S(2)}) async-start(), calls=%async_computation.2 | async-start | bytes 1310720 | tf_op jit(solution)/shard_map/all_gather | solution.py:44
  8.0 373.9 %copy-start.3 = (bf16[5,2048,32]{1,2,0:T(8,128)(2,1)S(1)}, bf16[5,2048,32]{1,2,0:T(8,128)(2,1)}, u32[]{:S(2)}) copy-start(bf16[5,2048,32]{1,2,0:T(8,128)(2,1)} %param.15) | copy-start | bytes 1966084
  357.9 91.4 %reduce-scatter.3.cloned.1.call-start = ((), (), s32[]{:S(2)}) async-start(), calls=%async_computation.3 | async-start | bytes 2621440 | tf_op jit(solution)/shard_map/reduce_scatter | solution.py:54
  383.4 5.4 collective-permute-start
  388.9 6.6 collective-permute-start.1
  395.5 5.4 collective-permute-start.2
  400.9 5.3 collective-permute-start.3
  406.2 8.0 collective-permute-start.4
  414.1 2.0 copy-start.7
  414.1 2.0 copy-start.8
  414.2 2.0 copy-start.1
  416.1 1.0 copy-start.5
  416.1 748.4 %all-gather.5.cloned.1.call-start = ((), (), s32[]{:S(2)}) async-start(), calls=%async_computation.4 | async-start | bytes 1310720 | tf_op jit(solution)/shard_map/all_gather | solution.py:44
  420.8 28.5 %copy-start.6 = (f32[512]{0:T(512)S(1)}, f32[512]{0:T(512)}, u32[]{:S(2)}) copy-start(f32[512]{0:T(512)} %param.10) | copy-start | bytes 6148
  421.8 742.7 %copy-start.4 = (bf16[5,2048,32]{1,2,0:T(8,128)(2,1)S(1)}, bf16[5,2048,32]{1,2,0:T(8,128)(2,1)}, u32[]{:S(2)}) copy-start(bf16[5,2048,32]{1,2,0:T(8,128)(2,1)} %param.15) | copy-start | bytes 1966084
  1144.3 87.8 %reduce-scatter.5.cloned.1.call-start = ((), (), s32[]{:S(2)}) async-start(), calls=%async_computation.5 | async-start | bytes 2621440 | tf_op jit(solution)/shard_map/reduce_scatter | solution.py:54
  1166.0 5.4 collective-permute-start.5
  1171.5 6.6 collective-permute-start.6
  1178.1 5.4 collective-permute-start.7
  1183.5 5.3 collective-permute-start.8
  1188.8 8.1 collective-permute-start.9
  1196.9 1.9 copy-start.2
Sparse Core Ops, SparseCore 0:
  358.0 23.7 all-gather.2
  416.2 33.0 reduce-scatter.2
  1144.4 20.0 all-gather.4
  1199.0 33.0 reduce-scatter.4
where the time goes:
time: 1940 us
  blocking collectives  1730 us (89%)
  waiting for transfers between devices  129 us (7%)
  starting transfers between devices  29.2 us (2%)
    psum x1, blocking collectives, local(): lax.psum(jnp.sum(rest_one * rest_one, axis=0), ('leaf', 'rank')) + EPSILON  348 us
    psum x1, blocking collectives, local(): lax.psum(jnp.sum(rest_two * rest_two, axis=0), ('leaf', 'rank')) + EPSILON  348 us
    psum x1, blocking collectives, local(): lax.psum(jnp.sum(start * start, axis=0), ('leaf', 'rank')) + EPSILON  346 us
    psum x1, blocking collectives, local(): lax.psum((jnp.sum(basis_one * image_two, axis=0), jnp.sum(basis_two * ima...  344 us
    psum x1, blocking collectives, local(): h11 = lax.psum(jnp.sum(basis_one * image_one, axis=0), ('leaf', 'rank'))  344 us
    reduce_scatter x2, waiting for transfers between devices, apply(): lax.psum_scatter(jnp.einsum('lpk,lkn->pn', gen_u, sibling, preferred_elem...  53 us
    all_gather x2, waiting for transfers between devices, apply(): subtree = lax.all_gather(narrow, 'rank', axis=0, tiled=True)  44 us
  transfers between devices with their start and end apart: 14, of which 14 were waited for; matrix products, arithmetic and copies ran while one was open for 1% of the time, Pallas kernels for 0%

commit v1 on v0

v1 whole, which is shorter than its diff:
```python
import functools

import jax
import jax.numpy as jnp
from jax import lax
from jax.experimental import pallas as pl
from jax.experimental.pallas import tpu as pltpu
from jax.sharding import PartitionSpec as P

EPSILON = 1e-06
MESH = pl.DeviceIdType.MESH
F32, BF16 = jnp.float32, jnp.bfloat16
BLK = 128
KEEP = 128
PLANE = [(dy, dx) for dy in range(4) for dx in range(4)]


def flip(value, bit):
    return value + bit - 2 * bit * lax.rem(lax.div(value, bit), 2)


def dot(a, b, contract=((1,), (0,))):
    return lax.dot_general(a, b, (contract, ((), ())), preferred_element_type=F32)


def kernel(
    order_ref, diag_ref, rows_ref, cols_ref, rhs_hbm, blocks_hbm, gu_hbm, gv_hbm, sol_ref, res_ref,
    s_ref, blk, vt, ut, pt, pm, vp, up, bm, xg, cs, dg, vec, img, img2,
    sb, l1b, l0b, r24, r1, r0, zs, zr, g24, g1, g0, cf24, cf1, cf0, ext0, ext1, ps, pr, pz, pzr,
    lsem, vsem, usem, s1s, s1r, s2s, s2r, s3s, s3r, nes, ner, qs, qr, zqs, zqr,
):
    leaf, y, core = (lax.axis_index(name) for name in ("leaf", "rank", "rhs"))
    x, z = lax.rem(leaf, 4), lax.div(leaf, 4)
    xs = [x, flip(x, 1), flip(x, 2), 3 - x]
    ys = [y] + [lax.rem(y + k, 4) for k in (1, 2, 3)]
    back = [y] + [lax.rem(y + 4 - k, 4) for k in (1, 2, 3)]
    zs_of = [z]
    for bit in (1, 2, 4):
        zs_of = zs_of + [flip(v, bit) for v in zs_of]
    slot = y * 4 + x
    slot1 = y * 2 + lax.rem(x, 2)
    sends = []

    def plane_id(dy, dx):
        return (z * 4 + xs[dx], ys[dy], core)

    def column_id(dz):
        return (zs_of[dz] * 4 + x, y, core)

    def remote(src, dst, send, recv, to):
        return pltpu.make_async_remote_copy(
            src_ref=src, dst_ref=dst, send_sem=send, recv_sem=recv, device_id=to, device_id_type=MESH
        )

    def push(*what):
        copy = remote(*what)
        copy.start()
        sends.append(copy)

    load_s = pltpu.make_async_copy(rhs_hbm, s_ref, lsem.at[0])
    load_b = pltpu.make_async_copy(blocks_hbm, blk, lsem.at[1])
    own_cols = pl.ds(pl.multiple_of(y * 512, 512), 512)
    load_v = pltpu.make_async_copy(gv_hbm.at[:, :, own_cols], vt.at[:, y], lsem.at[2])
    load_u = pltpu.make_async_copy(gu_hbm.at[:, :, own_cols], ut.at[:, y], lsem.at[3])
    for load in (load_s, load_v, load_b, load_u):
        load.start()

    barrier = pltpu.get_barrier_semaphore()
    peers = [plane_id(dy, dx) for dy, dx in PLANE[1:]] + [column_id(dz) for dz in range(1, 8)]
    for peer in peers:
        pl.semaphore_signal(barrier, inc=1, device_id=peer, device_id_type=MESH)

    ol = order_ref[...] - (leaf * 4 + y) * 512
    row = lax.broadcasted_iota(jnp.int32, (512, 512), 0)
    col = lax.broadcasted_iota(jnp.int32, (512, 512), 1)
    hit = row == ol
    dg[...] = jnp.broadcast_to(
        jnp.sum(jnp.where(hit, jnp.broadcast_to(diag_ref[...], (512, 512)), 0.0), axis=1, keepdims=True), (512, 256)
    )
    hot = jnp.where(hit, 1.0, 0.0).astype(BF16)
    for r in range(4):
        pt[r] = hot[:, r * BLK : (r + 1) * BLK]

    load_s.wait()
    s = s_ref[...]
    sq = s * s
    zero = jnp.zeros((1, 256), F32)

    def sum_start(i, values):
        ps[i] = jnp.concatenate(values + [zero] * (8 - len(values)), 0)
        for d, (dy, dx) in enumerate(PLANE):
            if d:
                push(ps.at[i], pr.at[i, d], qs.at[i, d], qr.at[i, d], plane_id(dy, dx))

    def sum_turn(i):
        total = ps[i]
        for d, (dy, dx) in enumerate(PLANE):
            if d:
                remote(ps.at[i], pr.at[i, d], qs.at[i, d], qr.at[i, d], plane_id(dy, dx)).wait_recv()
                total = total + pr[i, d]
        pz[i] = total
        for dz in range(1, 8):
            push(pz.at[i], pzr.at[i, dz], zqs.at[i, dz], zqr.at[i, dz], column_id(dz))

    def sum_end(i):
        total = pz[i]
        for dz in range(1, 8):
            remote(pz.at[i], pzr.at[i, dz], zqs.at[i, dz], zqr.at[i, dz], column_id(dz)).wait_recv()
            total = total + pzr[i, dz]
        return total

    def column_sum(value):
        return jnp.sum(value, axis=0, keepdims=True)

    first = [column_sum(sq), column_sum(dg[...] * sq)]
    pl.semaphore_wait(barrier, len(peers))

    def spread(gen, held, sems):
        for dy in (1, 3, 2):
            columns = pl.ds(pl.multiple_of(ys[dy] * 512, 512), 512)
            push(gen.at[:, :, columns], held.at[:, y], sems.at[0, dy], sems.at[1, dy], plane_id(dy, 0))

    def gathered(gen, held, sems):
        for dy in (1, 3, 2):
            remote(
                gen.at[:, :, pl.ds(0, 512)], held.at[:, back[dy]], sems.at[0, dy], sems.at[1, dy], plane_id(dy, 0)
            ).wait_recv()

    sum_start(0, first)
    spread(gv_hbm, vt, vsem)
    spread(gu_hbm, ut, usem)

    eye = jnp.where(row == col, 1.0, 0.0).astype(BF16)
    pm[...] = dot(eye, hot, ((1,), (1,))).astype(BF16)
    load_b.wait()
    for k in range(12):
        at = jnp.clip(rows_ref[k] - (leaf * 4 + y) * 4, 0, 3)
        bm[:, k * BLK : (k + 1) * BLK] = dot(pt[at], blk[k]).astype(BF16)
    sum_turn(0)
    load_v.wait()
    gathered(gv_hbm, vt, vsem)
    vp[...] = dot(vt[...].reshape(640, 512), pm[...]).astype(BF16)

    totals = sum_end(0)
    s_sum, d_sum = totals[0:1], totals[1:2]
    beta = jnp.sqrt(s_sum + EPSILON)
    inv_beta = 1.0 / beta
    shift = d_sum / (beta * beta)
    b1b1 = s_sum / (beta * beta)

    def apply_start(a, q, q_low=None):
        ext = (ext0, ext1)[a]
        ct = dot(vp[...], q)
        if q_low is not None:
            ct = ct + dot(vp[...], q_low)
        ct = ct.astype(BF16)
        for t in range(16):
            g, c = t // 2, t % 2
            for b in range(3):
                sb[a, t, b * 16 : b * 16 + 16] = ct[(b + 2) * KEEP + g * 16 :, c * 128 :][:16, :128]
        for d, (dy, dx) in enumerate(PLANE):
            if d:
                push(sb.at[a, ys[dy] * 4 + xs[dx]], r24.at[a, d], s1s.at[a, d], s1r.at[a, d], plane_id(dy, dx))
        for t in range(4):
            for c in range(2):
                l0b[a, t, c * 32 : c * 32 + 32] = ct[t * 32 :, c * 128 :][:32, :128]
        for dy in range(4):
            n = 16 + dy
            push(l0b.at[a, ys[dy]], r0.at[a, dy], s1s.at[a, n], s1r.at[a, n], plane_id(dy, 1))
        for t in range(8):
            for c in range(2):
                l1b[a, t, c * 16 : c * 16 + 16] = ct[KEEP + t * 16 :, c * 128 :][:16, :128]
        for dy in range(4):
            for dx in (2, 3):
                n, k = 20 + dy * 2 + dx - 2, dy * 2 + dx - 2
                there = ys[dy] * 2 + lax.rem(xs[dx], 2)
                push(l1b.at[a, there], r1.at[a, k], s1s.at[a, n], s1r.at[a, n], plane_id(dy, dx))
        ext[4:8] = dot(pm[...], q).astype(BF16).reshape(4, BLK, 256)
        push(ext.at[pl.ds(4, 4)], ext.at[pl.ds(0, 4)], nes.at[a, 0], ner.at[a, 0], plane_id(1, 0))
        push(ext.at[pl.ds(4, 4)], ext.at[pl.ds(8, 4)], nes.at[a, 1], ner.at[a, 1], plane_id(3, 0))

    def apply_end(a, out, before=None):
        ext = (ext0, ext1)[a]
        total = sb[a, slot].astype(F32)
        for d, (dy, dx) in enumerate(PLANE):
            if d:
                remote(sb.at[a, 0], r24.at[a, d], s1s.at[a, d], s1r.at[a, d], plane_id(dy, dx)).wait_recv()
                total = total + r24[a, d].astype(F32)
        zs[a] = total
        for dz in range(1, 8):
            b = 0 if dz < 2 else 1 if dz < 4 else 2
            push(zs.at[a, pl.ds(b * 16, 16)], zr.at[a, dz], s2s.at[a, dz], s2r.at[a, dz], column_id(dz))
        total = jnp.zeros((64, 128), F32)
        for dy in range(4):
            n = 16 + dy
            remote(l0b.at[a, 0], r0.at[a, dy], s1s.at[a, n], s1r.at[a, n], plane_id(dy, 1)).wait_recv()
            total = total + r0[a, dy].astype(F32)
        g0[a] = total.astype(BF16)
        cf0[a, y] = g0[a]
        for dy in range(1, 4):
            n = 16 + dy
            push(g0.at[a], cf0.at[a, y], s3s.at[a, n], s3r.at[a, n], plane_id(dy, 0))
        total = jnp.zeros((32, 128), F32)
        for dy in range(4):
            for dx in (2, 3):
                n, k = 20 + dy * 2 + dx - 2, dy * 2 + dx - 2
                remote(l1b.at[a, 0], r1.at[a, k], s1s.at[a, n], s1r.at[a, n], plane_id(dy, dx)).wait_recv()
                total = total + r1[a, k].astype(F32)
        g1[a] = total.astype(BF16)
        cf1[a, slot1] = g1[a]
        for dy in range(4):
            for dx in range(2):
                if dy or dx:
                    n = 20 + dy * 2 + dx
                    push(g1.at[a], cf1.at[a, slot1], s3s.at[a, n], s3r.at[a, n], plane_id(dy, dx))
        parts = []
        for b, group in enumerate(((1,), (2, 3), (4, 5, 6, 7))):
            total = jnp.zeros((16, 128), F32)
            for dz in group:
                remote(
                    zs.at[a, pl.ds(b * 16, 16)], zr.at[a, dz], s2s.at[a, dz], s2r.at[a, dz], column_id(dz)
                ).wait_recv()
                total = total + zr[a, dz]
            g24[a, b * 16 : b * 16 + 16] = total.astype(BF16)
        cf24[a, slot] = g24[a]
        for d, (dy, dx) in enumerate(PLANE):
            if d:
                push(g24.at[a], cf24.at[a, slot], s3s.at[a, d], s3r.at[a, d], plane_id(dy, dx))

        if before is not None:
            before()
        remote(
            ext.at[pl.ds(4, 4)], ext.at[pl.ds(0, 4)], nes.at[a, 0], ner.at[a, 0], plane_id(1, 0)
        ).wait_recv()
        remote(
            ext.at[pl.ds(4, 4)], ext.at[pl.ds(8, 4)], nes.at[a, 1], ner.at[a, 1], plane_id(3, 0)
        ).wait_recv()
        for k in range(12):
            at = jnp.clip(cols_ref[k] - (leaf * 4 + y) * 4 + 4, 0, 11)
            xg[k * BLK : (k + 1) * BLK] = ext[at]
        out[...] = dot(bm[...], xg[...])

        for dy in range(1, 4):
            n = 16 + dy
            remote(g0.at[a], cf0.at[a, back[dy]], s3s.at[a, n], s3r.at[a, n], plane_id(dy, 0)).wait_recv()
        for t in range(4):
            for c in range(2):
                cs[t * 32 : t * 32 + 32, c * 128 : c * 128 + 128] = cf0[a, t, c * 32 : c * 32 + 32]
        for dy in range(4):
            for dx in range(2):
                if dy or dx:
                    n = 20 + dy * 2 + dx
                    there = back[dy] * 2 + lax.rem(xs[dx], 2)
                    remote(g1.at[a], cf1.at[a, there], s3s.at[a, n], s3r.at[a, n], plane_id(dy, dx)).wait_recv()
        for t in range(8):
            for c in range(2):
                cs[KEEP + t * 16 : KEEP + t * 16 + 16, c * 128 : c * 128 + 128] = cf1[a, t, c * 16 : c * 16 + 16]
        out[...] += dot(up[:, : 2 * KEEP], cs[: 2 * KEEP])
        for d, (dy, dx) in enumerate(PLANE):
            if d:
                there = back[dy] * 4 + xs[dx]
                remote(g24.at[a], cf24.at[a, there], s3s.at[a, d], s3r.at[a, d], plane_id(dy, dx)).wait_recv()
        for t in range(16):
            g, c = t // 2, t % 2
            for b in range(3):
                at = (b + 2) * KEEP + g * 16
                cs[at : at + 16, c * 128 : c * 128 + 128] = cf24[a, t, b * 16 : b * 16 + 16]
        out[...] += dot(up[:, 2 * KEEP :], cs[2 * KEEP :])

    b1 = s * inv_beta
    apply_start(0, b1.astype(BF16))

    def own_u():
        load_u.wait()
        gathered(gu_hbm, ut, usem)
        hot_t = jnp.concatenate([pt[r] for r in range(4)], 1)
        up[...] = dot(hot_t, ut[...].reshape(640, 512), ((1,), (1,))).astype(BF16)

    apply_end(0, img, own_u)
    b1 = s_ref[...] * inv_beta
    p = (dg[...] - shift) * b1 + img[...]
    vec[...] = p
    q = p.astype(BF16)
    apply_start(1, q, (p - q.astype(F32)).astype(BF16))
    apply_end(1, img2)
    b1 = s_ref[...] * inv_beta
    p = vec[...]
    w = dg[...] * p + img2[...]
    img2[...] = w
    sum_start(1, [column_sum(v) for v in (b1 * p, p * p, b1 * w, p * w, w * w)])
    sum_turn(1)
    totals = sum_end(1)
    e, pp, f, g, ww = (totals[k : k + 1] for k in range(5))
    h11 = e + shift * b1b1
    delta = h11 - shift
    h21 = jnp.sqrt(jnp.maximum(pp - 2.0 * delta * e + delta * delta * b1b1, 0.0) + EPSILON)
    h12 = (f - delta * h11) / h21
    h22 = (g - delta * (pp + shift * e) - delta * f + delta * delta * h11) / (h21 * h21)
    of_w = 1.0 / h21
    of_p = -(delta + h22) / h21
    of_b = -(delta * shift / h21 + h12 - h22 * delta / h21)
    rest = (
        of_w * of_w * ww + of_p * of_p * pp + of_b * of_b * b1b1
        + 2.0 * (of_w * of_p * g + of_w * of_b * f + of_p * of_b * e)
    )
    h32 = jnp.sqrt(jnp.maximum(rest, 0.0) + EPSILON)
    r_one = jnp.sqrt(h11 * h11 + h21 * h21)
    cos_one = h11 / r_one
    sin_one = h21 / r_one
    top = cos_one * h12 + sin_one * h22
    low = cos_one * h22 - sin_one * h12
    r_two = jnp.sqrt(low * low + h32 * h32)
    y_two = low / r_two * (-sin_one * beta) / r_two
    y_one = (cos_one * beta - top * y_two) / r_one
    of_one = beta - y_one * h11 - y_two * h12
    of_two = -(y_one * h21 + y_two * h22)
    sol_ref[...] = (y_one - y_two * delta / h21) * b1 + (y_two / h21) * p
    res_ref[...] = (
        (of_one - of_two * delta / h21 - y_two * of_b) * b1
        + (of_two / h21 - y_two * of_p) * p
        - (y_two * of_w) * w
    )
    for copy in sends:
        copy.wait_send()


def local(rhs, order, diag, blocks, near_rows, near_cols, gen_u, gen_v):
    vmem, smem, hbm = (pl.BlockSpec(memory_space=m) for m in (pltpu.VMEM, pltpu.SMEM, pltpu.HBM))
    scratch = [
        ((512, 256), F32),
        ((12, BLK, BLK), BF16),
        ((5, 4, 32, 512), BF16),
        ((5, 4, 32, 512), BF16),
        ((4, 512, BLK), BF16),
        ((512, 512), BF16),
        ((640, 512), BF16),
        ((512, 640), BF16),
        ((512, 1536), BF16),
        ((1536, 256), BF16),
        ((640, 256), BF16),
        ((512, 256), F32),
        ((512, 256), F32),
        ((512, 256), F32),
        ((512, 256), F32),
        ((2, 16, 48, 128), BF16),
        ((2, 8, 32, 128), BF16),
        ((2, 4, 64, 128), BF16),
        ((2, 16, 48, 128), BF16),
        ((2, 8, 32, 128), BF16),
        ((2, 4, 64, 128), BF16),
        ((2, 48, 128), F32),
        ((2, 8, 16, 128), F32),
        ((2, 48, 128), BF16),
        ((2, 32, 128), BF16),
        ((2, 64, 128), BF16),
        ((2, 16, 48, 128), BF16),
        ((2, 8, 32, 128), BF16),
        ((2, 4, 64, 128), BF16),
        ((12, BLK, 256), BF16),
        ((12, BLK, 256), BF16),
        ((2, 8, 256), F32),
        ((2, 16, 8, 256), F32),
        ((2, 8, 256), F32),
        ((2, 8, 8, 256), F32),
    ]
    sems = [(4,), (2, 4), (2, 4), (2, 28), (2, 28), (2, 8), (2, 8), (2, 28), (2, 28), (2, 2), (2, 2), (2, 16), (2, 16), (2, 8), (2, 8)]
    return pl.pallas_call(
        kernel,
        out_shape=[jax.ShapeDtypeStruct(rhs.shape, F32)] * 2,
        in_specs=[vmem, vmem, smem, smem, hbm, hbm, hbm, hbm],
        out_specs=[vmem, vmem],
        scratch_shapes=[pltpu.VMEM(*s) for s in scratch] + [pltpu.SemaphoreType.DMA(s) for s in sems],
        compiler_params=pltpu.CompilerParams(
            collective_id=0, has_side_effects=True, vmem_limit_bytes=60 * 1024 * 1024
        ),
    )(
        order.reshape(1, -1), diag.reshape(1, -1), near_rows, near_cols, rhs, blocks,
        gen_u.transpose(0, 2, 1), gen_v.transpose(0, 2, 1),
    )


def solution(mesh):
    in_specs = (
        P(("leaf", "rank"), "rhs"),
        P(("leaf", "rank")),
        P(("leaf", "rank")),
        P(("leaf", "rank"), None, None),
        P(("leaf", "rank")),
        P(("leaf", "rank")),
        P(None, "leaf", "rank"),
        P(None, "leaf", "rank"),
    )
    out_specs = (P(("leaf", "rank"), "rhs"), P(("leaf", "rank"), "rhs"))
    return jax.shard_map(local, mesh=mesh, in_specs=in_specs, out_specs=out_specs, check_vma=False)
```

time: 1940 us -> 78.3 us (0.04)
  blocking collectives: 1730 us -> 0 us
  waiting for transfers between devices: 129 us -> 0 us
  Pallas kernels: 0 us -> 74.8 us
  starting transfers between devices: 29.2 us -> 0 us
    psum x5 -> x0, blocking collectives: 1730 us -> none  [the longest x1 348 us: local(): lax.psum(jnp.sum(rest_one * rest_one, axis=0), ('leaf', 'rank')) + EPSILON]
    pallas_call x0 -> x1, Pallas kernels: none -> 74.8 us  [local(): pl.pallas_call(kernel, out_shape=[jax.ShapeDtypeStruct(rhs.shape, F32)] *...]
    reduce_scatter x2 -> x0, waiting for transfers between devices: 53 us -> none  [apply(): lax.psum_scatter(jnp.einsum('lpk,lkn->pn', gen_u, sibling, preferred_elem...]
    all_gather x2 -> x0, waiting for transfers between devices: 44 us -> none  [apply(): subtree = lax.all_gather(narrow, 'rank', axis=0, tiled=True)]
    ppermute x10 -> x0, waiting for transfers between devices: 32.3 us -> none  [from_partner(): return lax.ppermute(value, axis, pairs)]
    ppermute x10 -> x0, starting transfers between devices: 29 us -> none  [from_partner(): return lax.ppermute(value, axis, pairs)]
  transfers between devices with their start and end apart: 14 -> 0, of which waited for: 14 -> 0; matrix products, arithmetic and copies ran while one was open for 1% -> 0% of each run, Pallas kernels for 0% -> 0%
where the time goes in v1:
time: 78.3 us; the launch traced here: 78.2 us
  Pallas kernels  74.8 us (96%)
  local copies, waits for them, and re-layouts  2.72 us (3%)
    pallas_call x1, Pallas kernels, local(): pl.pallas_call(kernel, out_shape=[jax.ShapeDtypeStruct(rhs.shape, F32)] *...  74.8 us
    unnamed x4, local copies, waits for them, and re-layouts  2.72 us

profile of v1, /device:TPU:8, one launch (start us, length us, event | category | flops | bytes accessed | tf_op | source)
XLA Modules:
  0.0 78.2 jit_solution(2065307702608617632)
XLA Ops:
  0.6 74.8 %shard_map.95 = (f32[512,256]{1,0:T(8,128)}, f32[512,256]{1,0:T(8,128)}) custom-call(s32[1,512]{1,0:T(1,128)} %bitcast.6, f32[1,512]{1,0:T(1,128)} %bitcast.7, s32[12]{0:T(128)} %rows_ref.1, s32[12]{0:T(128)} %cols_ref.1, f32[512,256]{1,0:T(8,128)} %rhs_hbm.1, bf16[12,128,128]{2,1,0:T(8,128)(2,1)} %blocks_hbm.1, bf16[5,32,2048]{2,1,0:T(8,128)(2,1)} %bitcast.4, ...), custom_call_target="tpu_custom_call" | custom-call | tf_op jit(solution)/shard_map/pallas_call | solution.py:367
  75.5 0.0 copy-start
  75.5 1.9 %copy.12 = f32[512,256]{1,0:T(8,128)} copy(f32[512,256]{1,0:T(8,128)} %get-tuple-element.4) | data formatting | bytes 1048576
  77.4 0.0 copy-done
  77.4 0.8 %copy.13 = f32[512,256]{1,0:T(8,128)} copy(f32[512,256]{1,0:T(8,128)S(1)} %copy-done) | data formatting | bytes 1048576
Async XLA Ops:
  75.5 1.9 %copy-start = (f32[512,256]{1,0:T(8,128)S(1)}, f32[512,256]{1,0:T(8,128)}, u32[]{:S(2)}) copy-start(f32[512,256]{1,0:T(8,128)} %get-tuple-element.5) | copy-start | bytes 1572868

commit v2 on v1

--- a/solution.py
+++ b/solution.py
@@ -12,6 +12,7 @@
 F32, BF16 = jnp.float32, jnp.bfloat16
 BLK = 128
 KEEP = 128
+ROOM, LAST = 40_000_000, 8_000_000
 PLANE = [(dy, dx) for dy in range(4) for dx in range(4)]
 
 
@@ -24,10 +25,10 @@
 
 
 def kernel(
-    order_ref, diag_ref, rows_ref, cols_ref, rhs_hbm, blocks_hbm, gu_hbm, gv_hbm, sol_ref, res_ref,
-    s_ref, blk, vt, ut, pt, pm, vp, up, bm, xg, cs, dg, vec, img, img2,
+    order_hbm, diag_hbm, rows_hbm, cols_hbm, rhs_hbm, blocks_hbm, gu_hbm, gv_hbm, vec, img2, c0, c1, c2, c3, c4,
+    order_ref, diag_ref, rows_ref, cols_ref, s_ref, blk, vt, ut, pt, pm, vp, up, bm, xg, cs, dg, img,
     sb, l1b, l0b, r24, r1, r0, zs, zr, g24, g1, g0, cf24, cf1, cf0, ext0, ext1, ps, pr, pz, pzr,
-    lsem, vsem, usem, s1s, s1r, s2s, s2r, s3s, s3r, nes, ner, qs, qr, zqs, zqr,
+    lsem, vsem, usem, vfsem, ufsem, s1s, s1r, s2s, s2r, s3s, s3r, nes, ner, qs, qr, zqs, zqr,
 ):
     leaf, y, core = (lax.axis_index(name) for name in ("leaf", "rank", "rhs"))
     x, z = lax.rem(leaf, 4), lax.div(leaf, 4)
@@ -39,6 +40,7 @@
         zs_of = zs_of + [flip(v, bit) for v in zs_of]
     slot = y * 4 + x
     slot1 = y * 2 + lax.rem(x, 2)
+    twin = (leaf, y, 1 - core)
     sends = []
 
     def plane_id(dy, dx):
@@ -57,19 +59,23 @@
         copy.start()
         sends.append(copy)
 
-    load_s = pltpu.make_async_copy(rhs_hbm, s_ref, lsem.at[0])
-    load_b = pltpu.make_async_copy(blocks_hbm, blk, lsem.at[1])
-    own_cols = pl.ds(pl.multiple_of(y * 512, 512), 512)
-    load_v = pltpu.make_async_copy(gv_hbm.at[:, :, own_cols], vt.at[:, y], lsem.at[2])
-    load_u = pltpu.make_async_copy(gu_hbm.at[:, :, own_cols], ut.at[:, y], lsem.at[3])
-    for load in (load_s, load_v, load_b, load_u):
-        load.start()
-
     barrier = pltpu.get_barrier_semaphore()
-    peers = [plane_id(dy, dx) for dy, dx in PLANE[1:]] + [column_id(dz) for dz in range(1, 8)]
+    peers = [plane_id(dy, dx) for dy, dx in PLANE[1:]] + [column_id(dz) for dz in range(1, 8)] + [twin]
     for peer in peers:
         pl.semaphore_signal(barrier, inc=1, device_id=peer, device_id_type=MESH)
 
+    own_cols = pl.ds(pl.multiple_of(y * 512, 512), 512)
+    pairs = (
+        (order_hbm, order_ref), (diag_hbm, diag_ref), (rhs_hbm, s_ref), (rows_hbm, rows_ref), (cols_hbm, cols_ref),
+        (blocks_hbm, blk), (gv_hbm.at[:, :, :, own_cols], vt.at[:, y]), (gu_hbm.at[:, :, :, own_cols], ut.at[:, y]),
+    )
+    loads = [pltpu.make_async_copy(src, dst, lsem.at[k]) for k, (src, dst) in enumerate(pairs)]
+    for load in loads:
+        load.start()
+    load_o, load_d, load_s, load_r, load_c, load_b, load_v, load_u = loads
+
+    load_o.wait()
+    load_d.wait()
     ol = order_ref[...] - (leaf * 4 + y) * 512
     row = lax.broadcasted_iota(jnp.int32, (512, 512), 0)
     col = lax.broadcasted_iota(jnp.int32, (512, 512), 1)
@@ -84,76 +90,89 @@
     load_s.wait()
     s = s_ref[...]
     sq = s * s
-    zero = jnp.zeros((1, 256), F32)
 
     def sum_start(i, values):
-        ps[i] = jnp.concatenate(values + [zero] * (8 - len(values)), 0)
-        for d, (dy, dx) in enumerate(PLANE):
-            if d:
-                push(ps.at[i], pr.at[i, d], qs.at[i, d], qr.at[i, d], plane_id(dy, dx))
+        rows = [v[:, c * 128 : c * 128 + 128] for v in values for c in range(2)]
+        ps[i, : len(rows)] = jnp.concatenate(rows, 0)
+        for d, (dy, dx) in enumerate(PLANE):
+            if d:
+                part = pl.ds(0, 8 * (1 + i))
+                push(ps.at[i, part], pr.at[i, d, part], qs.at[i, d], qr.at[i, d], plane_id(dy, dx))
 
     def sum_turn(i):
-        total = ps[i]
-        for d, (dy, dx) in enumerate(PLANE):
-            if d:
-                remote(ps.at[i], pr.at[i, d], qs.at[i, d], qr.at[i, d], plane_id(dy, dx)).wait_recv()
-                total = total + pr[i, d]
-        pz[i] = total
+        part = pl.ds(0, 8 * (1 + i))
+        total = ps[i, part]
+        for d, (dy, dx) in enumerate(PLANE):
+            if d:
+                remote(ps.at[i, part], pr.at[i, d, part], qs.at[i, d], qr.at[i, d], plane_id(dy, dx)).wait_recv()
+                total = total + pr[i, d, part]
+        pz[i, part] = total
         for dz in range(1, 8):
-            push(pz.at[i], pzr.at[i, dz], zqs.at[i, dz], zqr.at[i, dz], column_id(dz))
-
-    def sum_end(i):
-        total = pz[i]
+            push(pz.at[i, part], pzr.at[i, dz, part], zqs.at[i, dz], zqr.at[i, dz], column_id(dz))
+
+    def sum_end(i, count):
+        part = pl.ds(0, 8 * (1 + i))
+        total = pz[i, part]
         for dz in range(1, 8):
-            remote(pz.at[i], pzr.at[i, dz], zqs.at[i, dz], zqr.at[i, dz], column_id(dz)).wait_recv()
-            total = total + pzr[i, dz]
-        return total
+            remote(pz.at[i, part], pzr.at[i, dz, part], zqs.at[i, dz], zqr.at[i, dz], column_id(dz)).wait_recv()
+            total = total + pzr[i, dz, part]
+        return [jnp.concatenate([total[2 * k : 2 * k + 1], total[2 * k + 1 : 2 * k + 2]], 1) for k in range(count)]
 
     def column_sum(value):
         return jnp.sum(value, axis=0, keepdims=True)
 
+    ps[...] = jnp.zeros_like(ps)
     first = [column_sum(sq), column_sum(dg[...] * sq)]
     pl.semaphore_wait(barrier, len(peers))
 
     def spread(gen, held, sems):
         for dy in (1, 3, 2):
             columns = pl.ds(pl.multiple_of(ys[dy] * 512, 512), 512)
-            push(gen.at[:, :, columns], held.at[:, y], sems.at[0, dy], sems.at[1, dy], plane_id(dy, 0))
-
-    def gathered(gen, held, sems):
+            push(
+                gen.at[:, core, :, columns], held.at[:, y, core], sems.at[0, dy], sems.at[1, dy], plane_id(dy, 0)
+            )
+
+    def hand_on(gen, held, sems, on):
         for dy in (1, 3, 2):
+            mine = held.at[:, back[dy], core]
             remote(
-                gen.at[:, :, pl.ds(0, 512)], held.at[:, back[dy]], sems.at[0, dy], sems.at[1, dy], plane_id(dy, 0)
+                gen.at[:, core, :, pl.ds(0, 512)], mine, sems.at[0, dy], sems.at[1, dy], plane_id(dy, 0)
             ).wait_recv()
+            push(mine, mine, on.at[0, dy], on.at[1, dy], twin)
+
+    def gathered(held, on):
+        for dy in (1, 3, 2):
+            mine, other = held.at[:, back[dy], core], held.at[:, back[dy], 1 - core]
+            remote(mine, other, on.at[0, dy], on.at[1, dy], twin).wait_recv()
 
     sum_start(0, first)
     spread(gv_hbm, vt, vsem)
-    spread(gu_hbm, ut, usem)
 
     eye = jnp.where(row == col, 1.0, 0.0).astype(BF16)
     pm[...] = dot(eye, hot, ((1,), (1,))).astype(BF16)
     load_b.wait()
+    load_r.wait()
+    load_c.wait()
     for k in range(12):
         at = jnp.clip(rows_ref[k] - (leaf * 4 + y) * 4, 0, 3)
         bm[:, k * BLK : (k + 1) * BLK] = dot(pt[at], blk[k]).astype(BF16)
     sum_turn(0)
     load_v.wait()
-    gathered(gv_hbm, vt, vsem)
-    vp[...] = dot(vt[...].reshape(640, 512), pm[...]).astype(BF16)
-
-    totals = sum_end(0)
-    s_sum, d_sum = totals[0:1], totals[1:2]
+    hand_on(gv_hbm, vt, vsem, vfsem)
+    spread(gu_hbm, ut, usem)
+    gathered(vt, vfsem)
+    hot = jnp.concatenate([pt[r] for r in range(4)], 1)
+    vp[...] = dot(vt[...].reshape(640, 512), hot, ((1,), (1,))).astype(BF16)
+
+    s_sum, d_sum = sum_end(0, 2)
     beta = jnp.sqrt(s_sum + EPSILON)
     inv_beta = 1.0 / beta
     shift = d_sum / (beta * beta)
     b1b1 = s_sum / (beta * beta)
 
-    def apply_start(a, q, q_low=None):
+    def apply_start(a, q):
         ext = (ext0, ext1)[a]
-        ct = dot(vp[...], q)
-        if q_low is not None:
-            ct = ct + dot(vp[...], q_low)
-        ct = ct.astype(BF16)
+        ct = dot(vp[...], q).astype(BF16)
         for t in range(16):
             g, c = t // 2, t % 2
             for b in range(3):
@@ -179,7 +198,7 @@
         push(ext.at[pl.ds(4, 4)], ext.at[pl.ds(0, 4)], nes.at[a, 0], ner.at[a, 0], plane_id(1, 0))
         push(ext.at[pl.ds(4, 4)], ext.at[pl.ds(8, 4)], nes.at[a, 1], ner.at[a, 1], plane_id(3, 0))
 
-    def apply_end(a, out, before=None):
+    def apply_end(a, out, early=None, before=None):
         ext = (ext0, ext1)[a]
         total = sb[a, slot].astype(F32)
         for d, (dy, dx) in enumerate(PLANE):
@@ -190,6 +209,8 @@
         for dz in range(1, 8):
             b = 0 if dz < 2 else 1 if dz < 4 else 2
             push(zs.at[a, pl.ds(b * 16, 16)], zr.at[a, dz], s2s.at[a, dz], s2r.at[a, dz], column_id(dz))
+        if early is not None:
+            early()
         total = jnp.zeros((64, 128), F32)
         for dy in range(4):
             n = 16 + dy
@@ -272,16 +293,15 @@
 
     def own_u():
         load_u.wait()
-        gathered(gu_hbm, ut, usem)
+        gathered(ut, ufsem)
         hot_t = jnp.concatenate([pt[r] for r in range(4)], 1)
         up[...] = dot(hot_t, ut[...].reshape(640, 512), ((1,), (1,))).astype(BF16)
 
-    apply_end(0, img, own_u)
+    apply_end(0, img, lambda: hand_on(gu_hbm, ut, usem, ufsem), own_u)
     b1 = s_ref[...] * inv_beta
     p = (dg[...] - shift) * b1 + img[...]
     vec[...] = p
-    q = p.astype(BF16)
-    apply_start(1, q, (p - q.astype(F32)).astype(BF16))
+    apply_start(1, p.astype(BF16))
     apply_end(1, img2)
     b1 = s_ref[...] * inv_beta
     p = vec[...]
@@ -289,8 +309,7 @@
     img2[...] = w
     sum_start(1, [column_sum(v) for v in (b1 * p, p * p, b1 * w, p * w, w * w)])
     sum_turn(1)
-    totals = sum_end(1)
-    e, pp, f, g, ww = (totals[k : k + 1] for k in range(5))
+    e, pp, f, g, ww = sum_end(1, 5)
     h11 = e + shift * b1b1
     delta = h11 - shift
     h21 = jnp.sqrt(jnp.maximum(pp - 2.0 * delta * e + delta * delta * b1b1, 0.0) + EPSILON)
@@ -314,23 +333,41 @@
     y_one = (cos_one * beta - top * y_two) / r_one
     of_one = beta - y_one * h11 - y_two * h12
     of_two = -(y_one * h21 + y_two * h22)
-    sol_ref[...] = (y_one - y_two * delta / h21) * b1 + (y_two / h21) * p
-    res_ref[...] = (
-        (of_one - of_two * delta / h21 - y_two * of_b) * b1
-        + (of_two / h21 - y_two * of_p) * p
-        - (y_two * of_w) * w
-    )
+    rows = (
+        (y_one - y_two * delta / h21) * inv_beta,
+        y_two / h21,
+        (of_one - of_two * delta / h21 - y_two * of_b) * inv_beta,
+        of_two / h21 - y_two * of_p,
+        -(y_two * of_w),
+    )
+    for ref, value in zip((c0, c1, c2, c3, c4), rows):
+        ref[...] = value
     for copy in sends:
         copy.wait_send()
 
 
+def combine(rhs, vec, image, c0, c1, c2, c3, c4, sol_hbm, res_hbm, sol, res, sem):
+    copies = []
+    for k in range(4):
+        part = pl.ds(k * 128, 128)
+        r, v, m = rhs[part], vec[part], image[part]
+        sol[part] = c0[...] * r + c1[...] * v
+        copies.append(pltpu.make_async_copy(sol.at[part], sol_hbm.at[part], sem.at[0, k]))
+        copies[-1].start()
+        res[part] = c2[...] * r + c3[...] * v + c4[...] * m
+        copies.append(pltpu.make_async_copy(res.at[part], res_hbm.at[part], sem.at[1, k]))
+        copies[-1].start()
+    for copy in copies:
+        copy.wait()
+
+
 def local(rhs, order, diag, blocks, near_rows, near_cols, gen_u, gen_v):
-    vmem, smem, hbm = (pl.BlockSpec(memory_space=m) for m in (pltpu.VMEM, pltpu.SMEM, pltpu.HBM))
+    vmem, hbm = (pl.BlockSpec(memory_space=m) for m in (pltpu.VMEM, pltpu.HBM))
     scratch = [
         ((512, 256), F32),
         ((12, BLK, BLK), BF16),
-        ((5, 4, 32, 512), BF16),
-        ((5, 4, 32, 512), BF16),
+        ((5, 4, 2, 16, 512), BF16),
+        ((5, 4, 2, 16, 512), BF16),
         ((4, 512, BLK), BF16),
         ((512, 512), BF16),
         ((640, 512), BF16),
@@ -338,8 +375,6 @@
         ((512, 1536), BF16),
         ((1536, 256), BF16),
         ((640, 256), BF16),
-        ((512, 256), F32),
-        ((512, 256), F32),
         ((512, 256), F32),
         ((512, 256), F32),
         ((2, 16, 48, 128), BF16),
@@ -358,25 +393,40 @@
         ((2, 4, 64, 128), BF16),
         ((12, BLK, 256), BF16),
         ((12, BLK, 256), BF16),
-        ((2, 8, 256), F32),
-        ((2, 16, 8, 256), F32),
-        ((2, 8, 256), F32),
-        ((2, 8, 8, 256), F32),
+        ((2, 16, 128), F32),
+        ((2, 16, 16, 128), F32),
+        ((2, 16, 128), F32),
+        ((2, 8, 16, 128), F32),
     ]
-    sems = [(4,), (2, 4), (2, 4), (2, 28), (2, 28), (2, 8), (2, 8), (2, 28), (2, 28), (2, 2), (2, 2), (2, 16), (2, 16), (2, 8), (2, 8)]
-    return pl.pallas_call(
+    sems = [(8,), (2, 4), (2, 4), (2, 4), (2, 4), (2, 28), (2, 28), (2, 8), (2, 8), (2, 28), (2, 28), (2, 2), (2, 2), (2, 16), (2, 16), (2, 8), (2, 8)]
+    vec, image, *coef = pl.pallas_call(
         kernel,
-        out_shape=[jax.ShapeDtypeStruct(rhs.shape, F32)] * 2,
-        in_specs=[vmem, vmem, smem, smem, hbm, hbm, hbm, hbm],
-        out_specs=[vmem, vmem],
-        scratch_shapes=[pltpu.VMEM(*s) for s in scratch] + [pltpu.SemaphoreType.DMA(s) for s in sems],
+        out_shape=[jax.ShapeDtypeStruct(shape, F32) for shape in (rhs.shape,) * 2 + ((1, 256),) * 5],
+        in_specs=[hbm] * 8,
+        out_specs=[vmem] * 7,
+        scratch_shapes=[pltpu.VMEM((1, 512), jnp.int32), pltpu.VMEM((1, 512), F32)]
+        + [pltpu.SMEM((12,), jnp.int32)] * 2
+        + [pltpu.VMEM(*s) for s in scratch] + [pltpu.SemaphoreType.DMA(s) for s in sems],
         compiler_params=pltpu.CompilerParams(
-            collective_id=0, has_side_effects=True, vmem_limit_bytes=60 * 1024 * 1024
+            collective_id=0, has_side_effects=True, vmem_limit_bytes=ROOM
         ),
     )(
-        order.reshape(1, -1), diag.reshape(1, -1), near_rows, near_cols, rhs, blocks,
-        gen_u.transpose(0, 2, 1), gen_v.transpose(0, 2, 1),
-    )
+        *(
+            pltpu.with_memory_space_constraint(value, pltpu.HBM)
+            for value in (
+                order.reshape(1, -1), diag.reshape(1, -1), near_rows, near_cols, rhs, blocks,
+                gen_u.transpose(0, 2, 1).reshape(5, 2, 16, -1), gen_v.transpose(0, 2, 1).reshape(5, 2, 16, -1),
+            )
+        )
+    )
+    return pl.pallas_call(
+        combine,
+        out_shape=[jax.ShapeDtypeStruct(rhs.shape, F32)] * 2,
+        in_specs=[vmem] * 8,
+        out_specs=[hbm] * 2,
+        scratch_shapes=[pltpu.VMEM((512, 256), F32)] * 2 + [pltpu.SemaphoreType.DMA((2, 4))],
+        compiler_params=pltpu.CompilerParams(vmem_limit_bytes=LAST),
+    )(rhs, vec, image, *coef)
 
 
 def solution(mesh):

time: 78.3 us -> 69 us (0.88)
  Pallas kernels: 74.8 us -> 68.3 us
  local copies, waits for them, and re-layouts: 2.72 us -> 0.01 us
    pallas_call x1 -> x2, Pallas kernels: 74.8 us -> 68.3 us  [the longest x1 67.2 us: local(): pl.pallas_call(kernel, out_shape=[jax.ShapeDtypeStruct(shape, F32) for sh...]
    unnamed x4 -> x2, local copies, waits for them, and re-layouts: 2.72 us -> 0.01 us
where the time goes in v2:
time: 69 us; the launch traced here: 68.9 us
  Pallas kernels  68.3 us (99%)
    pallas_call x1, Pallas kernels, local(): pl.pallas_call(kernel, out_shape=[jax.ShapeDtypeStruct(shape, F32) for sh...  67.2 us

profile of v2, /device:TPU:8, one launch (start us, length us, event | category | flops | bytes accessed | tf_op | source)
XLA Modules:
  0.0 68.9 jit_solution(14770300123203039323)
XLA Ops:
  0.6 0.0 copy-start
  0.6 67.2 %shard_map.95 = (f32[512,256]{1,0:T(8,128)S(1)}, f32[512,256]{1,0:T(8,128)S(1)}, f32[1,256]{1,0:T(1,128)S(1)}, f32[1,256]{1,0:T(1,128)S(1)}, f32[1,256]{1,0:T(1,...) custom-call(s32[1,512]{1,0:T(1,128)} %bitcast.10, f32[1,512]{1,0:T(1,128)} %bitcast.11, s32[12]{0:T(128)} %rows_hbm.1, ...), custom_call_target="tpu_custom_call" | custom-call | tf_op jit(solution)/shard_map/pallas_call | solution.py:402
  67.9 0.0 copy-done
  67.9 1.0 %shard_map.96 = (f32[512,256]{1,0:T(8,128)}, f32[512,256]{1,0:T(8,128)}) custom-call(f32[512,256]{1,0:T(8,128)S(1)} %copy-done, f32[512,256]{1,0:T(8,128)S(1)} %get-tuple-element.9.vec, f32[512,256]{1,0:T(8,128)S(1)} %get-tuple-element.10.image, f32[1,256]{1,0:T(1,128)S(1)} %get-tuple-element.11.c0, f32[1,256]{1,0:T(1,128)S(1)} %get-tuple-element.12.c1, ...), custom_call_target="tpu_custom_call" | custom-call | tf_op jit(solution)/shard_map/pallas_call | solution.py:422
Async XLA Ops:
  0.6 67.2 %copy-start = (f32[512,256]{1,0:T(8,128)S(1)}, f32[512,256]{1,0:T(8,128)}, u32[]{:S(2)}) copy-start(f32[512,256]{1,0:T(8,128)} %rhs.1) | copy-start | bytes 1572868

commit v3 on v2

--- a/solution.py
+++ b/solution.py
@@ -13,7 +13,10 @@
 BLK = 128
 KEEP = 128
 ROOM, LAST = 40_000_000, 8_000_000
+HOPS = (0, 1, 2, 1)
 PLANE = [(dy, dx) for dy in range(4) for dx in range(4)]
+FAR = sorted(range(1, 16), key=lambda d: -HOPS[d // 4] - HOPS[d % 4])
+FAR_Z = (4, 5, 7, 3, 6, 2, 1)
 
 
 def flip(value, bit):
@@ -27,8 +30,8 @@
 def kernel(
     order_hbm, diag_hbm, rows_hbm, cols_hbm, rhs_hbm, blocks_hbm, gu_hbm, gv_hbm, vec, img2, c0, c1, c2, c3, c4,
     order_ref, diag_ref, rows_ref, cols_ref, s_ref, blk, vt, ut, pt, pm, vp, up, bm, xg, cs, dg, img,
-    sb, l1b, l0b, r24, r1, r0, zs, zr, g24, g1, g0, cf24, cf1, cf0, ext0, ext1, ps, pr, pz, pzr,
-    lsem, vsem, usem, vfsem, ufsem, s1s, s1r, s2s, s2r, s3s, s3r, nes, ner, qs, qr, zqs, zqr,
+    sb4, sb, l1b, l0b, r4, r24, r1, r0, zs, zr, g4, g24, g1, g0, cf4, cf24, cf1, cf0, ext0, ext1, ps, pr, pz, pzr,
+    lsem, vsem, usem, vfsem, ufsem, s1s, s1r, s2s, s2r, s3s, s3r, s4s, s4r, s5s, s5r, nes, ner, qs, qr, zqs, zqr,
 ):
     leaf, y, core = (lax.axis_index(name) for name in ("leaf", "rank", "rhs"))
     x, z = lax.rem(leaf, 4), lax.div(leaf, 4)
@@ -94,24 +97,23 @@
     def sum_start(i, values):
         rows = [v[:, c * 128 : c * 128 + 128] for v in values for c in range(2)]
         ps[i, : len(rows)] = jnp.concatenate(rows, 0)
-        for d, (dy, dx) in enumerate(PLANE):
-            if d:
-                part = pl.ds(0, 8 * (1 + i))
-                push(ps.at[i, part], pr.at[i, d, part], qs.at[i, d], qr.at[i, d], plane_id(dy, dx))
+        part = pl.ds(0, 8 + 8 * i)
+        for d in FAR:
+            push(ps.at[i, part], pr.at[i, d, part], qs.at[i, d], qr.at[i, d], plane_id(*PLANE[d]))
 
     def sum_turn(i):
-        part = pl.ds(0, 8 * (1 + i))
+        part = pl.ds(0, 8 + 8 * i)
         total = ps[i, part]
         for d, (dy, dx) in enumerate(PLANE):
             if d:
                 remote(ps.at[i, part], pr.at[i, d, part], qs.at[i, d], qr.at[i, d], plane_id(dy, dx)).wait_recv()
                 total = total + pr[i, d, part]
         pz[i, part] = total
-        for dz in range(1, 8):
+        for dz in FAR_Z:
             push(pz.at[i, part], pzr.at[i, dz, part], zqs.at[i, dz], zqr.at[i, dz], column_id(dz))
 
     def sum_end(i, count):
-        part = pl.ds(0, 8 * (1 + i))
+        part = pl.ds(0, 8 + 8 * i)
         total = pz[i, part]
         for dz in range(1, 8):
             remote(pz.at[i, part], pzr.at[i, dz, part], zqs.at[i, dz], zqr.at[i, dz], column_id(dz)).wait_recv()
@@ -172,14 +174,21 @@
 
     def apply_start(a, q):
         ext = (ext0, ext1)[a]
-        ct = dot(vp[...], q).astype(BF16)
+        ct = dot(vp[4 * KEEP :], q).astype(BF16)
         for t in range(16):
             g, c = t // 2, t % 2
-            for b in range(3):
+            sb4[a, t] = ct[g * 16 :, c * 128 :][:16, :128]
+        for d in FAR:
+            dy, dx = PLANE[d]
+            push(sb4.at[a, ys[dy] * 4 + xs[dx]], r4.at[a, d], s4s.at[a, d], s4r.at[a, d], plane_id(dy, dx))
+        ct = dot(vp[: 4 * KEEP], q).astype(BF16)
+        for t in range(16):
+            g, c = t // 2, t % 2
+            for b in range(2):
                 sb[a, t, b * 16 : b * 16 + 16] = ct[(b + 2) * KEEP + g * 16 :, c * 128 :][:16, :128]
-        for d, (dy, dx) in enumerate(PLANE):
-            if d:
-                push(sb.at[a, ys[dy] * 4 + xs[dx]], r24.at[a, d], s1s.at[a, d], s1r.at[a, d], plane_id(dy, dx))
+        for d in FAR:
+            dy, dx = PLANE[d]
+            push(sb.at[a, ys[dy] * 4 + xs[dx]], r24.at[a, d], s1s.at[a, d], s1r.at[a, d], plane_id(dy, dx))
         for t in range(4):
             for c in range(2):
                 l0b[a, t, c * 32 : c * 32 + 32] = ct[t * 32 :, c * 128 :][:32, :128]
@@ -200,15 +209,27 @@
 
     def apply_end(a, out, early=None, before=None):
         ext = (ext0, ext1)[a]
+        total = sb4[a, slot].astype(F32)
+        for d, (dy, dx) in enumerate(PLANE):
+            if d:
+                remote(sb4.at[a, 0], r4.at[a, d], s4s.at[a, d], s4r.at[a, d], plane_id(dy, dx)).wait_recv()
+                total = total + r4[a, d].astype(F32)
+        zs[a, 32:48] = total
+
+        def push_z(dz):
+            b = 0 if dz < 2 else 1 if dz < 4 else 2
+            push(zs.at[a, pl.ds(b * 16, 16)], zr.at[a, dz], s2s.at[a, dz], s2r.at[a, dz], column_id(dz))
+
+        for dz in (4, 5, 7, 6):
+            push_z(dz)
         total = sb[a, slot].astype(F32)
         for d, (dy, dx) in enumerate(PLANE):
             if d:
                 remote(sb.at[a, 0], r24.at[a, d], s1s.at[a, d], s1r.at[a, d], plane_id(dy, dx)).wait_recv()
                 total = total + r24[a, d].astype(F32)
-        zs[a] = total
-        for dz in range(1, 8):
-            b = 0 if dz < 2 else 1 if dz < 4 else 2
-            push(zs.at[a, pl.ds(b * 16, 16)], zr.at[a, dz], s2s.at[a, dz], s2r.at[a, dz], column_id(dz))
+        zs[a, 0:32] = total
+        for dz in (3, 2, 1):
+            push_z(dz)
         if early is not None:
             early()
         total = jnp.zeros((64, 128), F32)
@@ -234,19 +255,24 @@
                 if dy or dx:
                     n = 20 + dy * 2 + dx
                     push(g1.at[a], cf1.at[a, slot1], s3s.at[a, n], s3r.at[a, n], plane_id(dy, dx))
-        parts = []
-        for b, group in enumerate(((1,), (2, 3), (4, 5, 6, 7))):
+        def sibling(b, group):
             total = jnp.zeros((16, 128), F32)
             for dz in group:
                 remote(
                     zs.at[a, pl.ds(b * 16, 16)], zr.at[a, dz], s2s.at[a, dz], s2r.at[a, dz], column_id(dz)
                 ).wait_recv()
                 total = total + zr[a, dz]
-            g24[a, b * 16 : b * 16 + 16] = total.astype(BF16)
+            return total.astype(BF16)
+
+        g4[a] = sibling(2, (6, 7, 5, 4))
+        for d in FAR:
+            push(g4.at[a], cf4.at[a, slot], s5s.at[a, d], s5r.at[a, d], plane_id(*PLANE[d]))
+        g24[a, 0:16] = sibling(0, (1,))
+        g24[a, 16:32] = sibling(1, (2, 3))
+        for d in FAR:
+            push(g24.at[a], cf24.at[a, slot], s3s.at[a, d], s3r.at[a, d], plane_id(*PLANE[d]))
+        cf4[a, slot] = g4[a]
         cf24[a, slot] = g24[a]
-        for d, (dy, dx) in enumerate(PLANE):
-            if d:
-                push(g24.at[a], cf24.at[a, slot], s3s.at[a, d], s3r.at[a, d], plane_id(dy, dx))
 
         if before is not None:
             before()
@@ -280,10 +306,18 @@
         for d, (dy, dx) in enumerate(PLANE):
             if d:
                 there = back[dy] * 4 + xs[dx]
+                remote(g4.at[a], cf4.at[a, there], s5s.at[a, d], s5r.at[a, d], plane_id(dy, dx)).wait_recv()
+        for t in range(16):
+            g, c = t // 2, t % 2
+            at = 4 * KEEP + g * 16
+            cs[at : at + 16, c * 128 : c * 128 + 128] = cf4[a, t]
+        for d, (dy, dx) in enumerate(PLANE):
+            if d:
+                there = back[dy] * 4 + xs[dx]
                 remote(g24.at[a], cf24.at[a, there], s3s.at[a, d], s3r.at[a, d], plane_id(dy, dx)).wait_recv()
         for t in range(16):
             g, c = t // 2, t % 2
-            for b in range(3):
+            for b in range(2):
                 at = (b + 2) * KEEP + g * 16
                 cs[at : at + 16, c * 128 : c * 128 + 128] = cf24[a, t, b * 16 : b * 16 + 16]
         out[...] += dot(up[:, 2 * KEEP :], cs[2 * KEEP :])
@@ -306,8 +340,11 @@
     b1 = s_ref[...] * inv_beta
     p = vec[...]
     w = dg[...] * p + img2[...]
+    sum_start(1, [column_sum(v) for v in (b1 * p, p * p, b1 * w, p * w, w * w)])
     img2[...] = w
-    sum_start(1, [column_sum(v) for v in (b1 * p, p * p, b1 * w, p * w, w * w)])
+    done = len(sends)
+    for copy in sends:
+        copy.wait_send()
     sum_turn(1)
     e, pp, f, g, ww = sum_end(1, 5)
     h11 = e + shift * b1b1
@@ -342,7 +379,7 @@
     )
     for ref, value in zip((c0, c1, c2, c3, c4), rows):
         ref[...] = value
-    for copy in sends:
+    for copy in sends[done:]:
         copy.wait_send()
 
 
@@ -377,18 +414,22 @@
         ((640, 256), BF16),
         ((512, 256), F32),
         ((512, 256), F32),
-        ((2, 16, 48, 128), BF16),
+        ((2, 16, 16, 128), BF16),
+        ((2, 16, 32, 128), BF16),
         ((2, 8, 32, 128), BF16),
         ((2, 4, 64, 128), BF16),
-        ((2, 16, 48, 128), BF16),
+        ((2, 16, 16, 128), BF16),
+        ((2, 16, 32, 128), BF16),
         ((2, 8, 32, 128), BF16),
         ((2, 4, 64, 128), BF16),
         ((2, 48, 128), F32),
         ((2, 8, 16, 128), F32),
-        ((2, 48, 128), BF16),
+        ((2, 16, 128), BF16),
+        ((2, 32, 128), BF16),
         ((2, 32, 128), BF16),
         ((2, 64, 128), BF16),
-        ((2, 16, 48, 128), BF16),
+        ((2, 16, 16, 128), BF16),
+        ((2, 16, 32, 128), BF16),
         ((2, 8, 32, 128), BF16),
         ((2, 4, 64, 128), BF16),
         ((12, BLK, 256), BF16),
@@ -398,7 +439,9 @@
         ((2, 16, 128), F32),
         ((2, 8, 16, 128), F32),
     ]
-    sems = [(8,), (2, 4), (2, 4), (2, 4), (2, 4), (2, 28), (2, 28), (2, 8), (2, 8), (2, 28), (2, 28), (2, 2), (2, 2), (2, 16), (2, 16), (2, 8), (2, 8)]
+    sems = [(8,), (2, 4), (2, 4), (2, 4), (2, 4)]
+    sems += [(2, 28), (2, 28), (2, 8), (2, 8), (2, 28), (2, 28), (2, 16), (2, 16), (2, 16), (2, 16)]
+    sems += [(2, 2), (2, 2), (2, 16), (2, 16), (2, 8), (2, 8)]
     vec, image, *coef = pl.pallas_call(
         kernel,
         out_shape=[jax.ShapeDtypeStruct(shape, F32) for shape in (rhs.shape,) * 2 + ((1, 256),) * 5],

time: 69 us -> 66.8 us (0.968)
  Pallas kernels: 68.3 us -> 66 us
    pallas_call x1, Pallas kernels: 67.2 us -> 64.9 us  [local(): pl.pallas_call(kernel, out_shape=[jax.ShapeDtypeStruct(shape, F32) for sh...]
where the time goes in v3:
time: 66.8 us; the launch traced here: 66.7 us
  Pallas kernels  66 us (99%)
    pallas_call x1, Pallas kernels, local(): pl.pallas_call(kernel, out_shape=[jax.ShapeDtypeStruct(shape, F32) for sh...  64.9 us

profile of v3, /device:TPU:8, one launch (start us, length us, event | category | flops | bytes accessed | tf_op | source)
XLA Modules:
  0.0 66.7 jit_solution(15612440675451310199)
XLA Ops:
  0.6 0.0 copy-start
  0.6 64.9 %shard_map.95 = (f32[512,256]{1,0:T(8,128)S(1)}, f32[512,256]{1,0:T(8,128)S(1)}, f32[1,256]{1,0:T(1,128)S(1)}, f32[1,256]{1,0:T(1,128)S(1)}, f32[1,256]{1,0:T(1,...) custom-call(s32[1,512]{1,0:T(1,128)} %bitcast.10, f32[1,512]{1,0:T(1,128)} %bitcast.11, s32[12]{0:T(128)} %rows_hbm.1, ...), custom_call_target="tpu_custom_call" | custom-call | tf_op jit(solution)/shard_map/pallas_call | solution.py:445
  65.6 0.0 copy-done
  65.6 1.0 %shard_map.96 = (f32[512,256]{1,0:T(8,128)}, f32[512,256]{1,0:T(8,128)}) custom-call(f32[512,256]{1,0:T(8,128)S(1)} %copy-done, f32[512,256]{1,0:T(8,128)S(1)} %get-tuple-element.9.vec, f32[512,256]{1,0:T(8,128)S(1)} %get-tuple-element.10.image, f32[1,256]{1,0:T(1,128)S(1)} %get-tuple-element.11.c0, f32[1,256]{1,0:T(1,128)S(1)} %get-tuple-element.12.c1, ...), custom_call_target="tpu_custom_call" | custom-call | tf_op jit(solution)/shard_map/pallas_call | solution.py:465
Async XLA Ops:
  0.6 65.0 %copy-start = (f32[512,256]{1,0:T(8,128)S(1)}, f32[512,256]{1,0:T(8,128)}, u32[]{:S(2)}) copy-start(f32[512,256]{1,0:T(8,128)} %rhs.1) | copy-start | bytes 1572868

commit v4 on v3

v4 whole, which is shorter than its diff:
```python
import functools

import jax
import jax.numpy as jnp
from jax import lax
from jax.experimental import pallas as pl
from jax.experimental.pallas import tpu as pltpu
from jax.sharding import PartitionSpec as P

EPSILON = 1e-06
MESH = pl.DeviceIdType.MESH
F32, BF16 = jnp.float32, jnp.bfloat16
BLK = 128
KEEP = 128
ROOM, LAST = 40_000_000, 8_000_000
HOPS = (0, 1, 2, 1)
PLANE = [(dy, dx) for dy in range(4) for dx in range(4)]
FAR = sorted(range(1, 16), key=lambda d: -HOPS[d // 4] - HOPS[d % 4])
FAR_Z = (4, 5, 7, 3, 6, 2, 1)


def flip(value, bit):
    return value + bit - 2 * bit * lax.rem(lax.div(value, bit), 2)


def dot(a, b, contract=((1,), (0,))):
    return lax.dot_general(a, b, (contract, ((), ())), preferred_element_type=F32)


def kernel(
    order_hbm, diag_hbm, rows_hbm, cols_hbm, rhs_hbm, blocks_hbm, gu_hbm, gv_hbm, vec, img2, c0, c1, c2, c3, c4,
    order_ref, diag_ref, rows_ref, cols_ref, s_ref, blk, vt, ut, pt, pm, vp, up, bm, xg, cs, dg, img,
    sb4, sb, l1b, l0b, r4, r24, r1, r0, zs, zr, g4, g24, g1, g0, cf4, cf24, cf1, cf0, ext0, ext1, ps, pr, pz, pzr,
    sem,
):
    leaf, y, core = (lax.axis_index(name) for name in ("leaf", "rank", "rhs"))
    x, z = lax.rem(leaf, 4), lax.div(leaf, 4)
    xs = [x, flip(x, 1), flip(x, 2), 3 - x]
    ys = [y] + [lax.rem(y + k, 4) for k in (1, 2, 3)]
    back = [y] + [lax.rem(y + 4 - k, 4) for k in (1, 2, 3)]
    zs_of = [z]
    for bit in (1, 2, 4):
        zs_of = zs_of + [flip(v, bit) for v in zs_of]
    slot = y * 4 + x
    slot1 = y * 2 + lax.rem(x, 2)
    twin = (leaf, y, 1 - core)
    sends = []

    def plane_id(dy, dx):
        return (z * 4 + xs[dx], ys[dy], core)

    def column_id(dz):
        return (zs_of[dz] * 4 + x, y, core)

    def remote(src, dst, send, recv, to):
        return pltpu.make_async_remote_copy(
            src_ref=src, dst_ref=dst, send_sem=send, recv_sem=recv, device_id=to, device_id_type=MESH
        )

    def push(*what):
        remote(*what).start()

    taken = []

    def fresh(count):
        first = len(taken)
        taken.extend(range(count))
        return [sem.at[first + k] for k in range(count)]

    def drain(ref, done):
        pltpu.make_async_copy(ref, ref, done).wait()

    barrier = pltpu.get_barrier_semaphore()
    peers = [plane_id(dy, dx) for dy, dx in PLANE[1:]] + [column_id(dz) for dz in range(1, 8)] + [twin]
    for peer in peers:
        pl.semaphore_signal(barrier, inc=1, device_id=peer, device_id_type=MESH)

    own_cols = pl.ds(pl.multiple_of(y * 512, 512), 512)
    pairs = (
        (order_hbm, order_ref), (diag_hbm, diag_ref), (rhs_hbm, s_ref), (rows_hbm, rows_ref), (cols_hbm, cols_ref),
        (blocks_hbm, blk), (gv_hbm.at[:, :, :, own_cols], vt.at[:, y]), (gu_hbm.at[:, :, :, own_cols], ut.at[:, y]),
    )
    loads = [pltpu.make_async_copy(src, dst, done) for (src, dst), done in zip(pairs, fresh(8))]
    for load in loads:
        load.start()
    load_o, load_d, load_s, load_r, load_c, load_b, load_v, load_u = loads

    load_o.wait()
    load_d.wait()
    ol = order_ref[...] - (leaf * 4 + y) * 512
    row = lax.broadcasted_iota(jnp.int32, (512, 512), 0)
    col = lax.broadcasted_iota(jnp.int32, (512, 512), 1)
    hit = row == ol
    dg[...] = jnp.broadcast_to(
        jnp.sum(jnp.where(hit, jnp.broadcast_to(diag_ref[...], (512, 512)), 0.0), axis=1, keepdims=True), (512, 256)
    )
    hot = jnp.where(hit, 1.0, 0.0).astype(BF16)
    for r in range(4):
        pt[r] = hot[:, r * BLK : (r + 1) * BLK]

    load_s.wait()
    s = s_ref[...]
    sq = s * s

    sum_sems = [fresh(4), fresh(4)]

    def sum_start(i, values):
        rows = [v[:, c * 128 : c * 128 + 128] for v in values for c in range(2)]
        ps[i, : len(rows)] = jnp.concatenate(rows, 0)
        part, (sent, got, _, _) = pl.ds(0, 8 + 8 * i), sum_sems[i]
        for d in FAR:
            push(ps.at[i, part], pr.at[i, d, part], sent, got, plane_id(*PLANE[d]))
        sends.append((pr.at[i, pl.ds(1, 15), part], sent))

    def sum_turn(i):
        part, (_, got, sent, _) = pl.ds(0, 8 + 8 * i), sum_sems[i]
        drain(pr.at[i, pl.ds(1, 15), part], got)
        total = ps[i, part]
        for d in range(1, 16):
            total = total + pr[i, d, part]
        pz[i, part] = total
        for dz in FAR_Z:
            push(pz.at[i, part], pzr.at[i, dz, part], sent, sum_sems[i][3], column_id(dz))
        sends.append((pzr.at[i, pl.ds(1, 7), part], sent))

    def sum_end(i, count):
        part = pl.ds(0, 8 + 8 * i)
        drain(pzr.at[i, pl.ds(1, 7), part], sum_sems[i][3])
        total = pz[i, part]
        for dz in range(1, 8):
            total = total + pzr[i, dz, part]
        return [total[2 * k : 2 * k + 2] for k in range(count)]

    def wide(value):
        return jnp.concatenate([value[0:1], value[1:2]], 1)

    def column_sum(value):
        return jnp.sum(value, axis=0, keepdims=True)

    ps[...] = jnp.zeros_like(ps)
    first = [column_sum(sq), column_sum(dg[...] * sq)]
    pl.semaphore_wait(barrier, len(peers))

    v_sems, u_sems = fresh(6), fresh(6)

    def spread(gen, held, sems):
        for k, dy in enumerate((1, 3, 2)):
            columns = pl.ds(pl.multiple_of(ys[dy] * 512, 512), 512)
            push(gen.at[:, core, :, columns], held.at[:, y, core], sems[3], sems[k], plane_id(dy, 0))
        sends.append((held.at[:, pl.ds(0, 3), core], sems[3]))

    def hand_on(gen, held, sems):
        for k, dy in enumerate((1, 3, 2)):
            mine = held.at[:, back[dy], core]
            drain(mine, sems[k])
            push(mine, mine, sems[4], sems[5], twin)
        sends.append((held.at[:, pl.ds(0, 3), core], sems[4]))

    def gathered(held, sems):
        drain(held.at[:, pl.ds(0, 3), 1 - core], sems[5])

    sum_start(0, first)
    spread(gv_hbm, vt, v_sems)

    eye = jnp.where(row == col, 1.0, 0.0).astype(BF16)
    pm[...] = dot(eye, hot, ((1,), (1,))).astype(BF16)
    load_b.wait()
    load_r.wait()
    load_c.wait()
    for k in range(12):
        at = jnp.clip(rows_ref[k] - (leaf * 4 + y) * 4, 0, 3)
        bm[:, k * BLK : (k + 1) * BLK] = dot(pt[at], blk[k]).astype(BF16)
    sum_turn(0)
    hand_on(gv_hbm, vt, v_sems)
    spread(gu_hbm, ut, u_sems)
    load_v.wait()
    gathered(vt, v_sems)
    vp[...] = dot(vt[...].reshape(640, 512), hot, ((1,), (1,))).astype(BF16)

    s_sum, d_sum = sum_end(0, 2)
    beta = jnp.sqrt(s_sum + EPSILON)
    inv_beta = 1.0 / beta
    inv_wide = wide(inv_beta)
    shift = d_sum / (beta * beta)
    b1b1 = s_sum / (beta * beta)

    stage_sems = [[fresh(2) for _ in range(11)] for _ in range(2)]

    def apply_start(a, q):
        four, pair, zero, one, _, _, _, _, _, _, near = stage_sems[a]
        ext = (ext0, ext1)[a]
        ct = dot(vp[4 * KEEP :], q).astype(BF16)
        for t in range(16):
            g, c = t // 2, t % 2
            sb4[a, t] = ct[g * 16 :, c * 128 :][:16, :128]
        for d in FAR:
            dy, dx = PLANE[d]
            push(sb4.at[a, ys[dy] * 4 + xs[dx]], r4.at[a, d], *four, plane_id(dy, dx))
        sends.append((r4.at[a, pl.ds(1, 15)], four[0]))
        ct = dot(vp[: 4 * KEEP], q).astype(BF16)
        for t in range(16):
            g, c = t // 2, t % 2
            for b in range(2):
                sb[a, t, b * 16 : b * 16 + 16] = ct[(b + 2) * KEEP + g * 16 :, c * 128 :][:16, :128]
        for d in FAR:
            dy, dx = PLANE[d]
            push(sb.at[a, ys[dy] * 4 + xs[dx]], r24.at[a, d], *pair, plane_id(dy, dx))
        sends.append((r24.at[a, pl.ds(1, 15)], pair[0]))
        for t in range(4):
            for c in range(2):
                l0b[a, t, c * 32 : c * 32 + 32] = ct[t * 32 :, c * 128 :][:32, :128]
        for dy in range(4):
            push(l0b.at[a, ys[dy]], r0.at[a, dy], *zero, plane_id(dy, 1))
        sends.append((r0.at[a], zero[0]))
        for t in range(8):
            for c in range(2):
                l1b[a, t, c * 16 : c * 16 + 16] = ct[KEEP + t * 16 :, c * 128 :][:16, :128]
        for dy in range(4):
            for dx in (2, 3):
                there = ys[dy] * 2 + lax.rem(xs[dx], 2)
                push(l1b.at[a, there], r1.at[a, dy * 2 + dx - 2], *one, plane_id(dy, dx))
        sends.append((r1.at[a], one[0]))
        ext[4:8] = dot(pm[...], q).astype(BF16).reshape(4, BLK, 256)
        push(ext.at[pl.ds(4, 4)], ext.at[pl.ds(0, 4)], *near, plane_id(1, 0))
        push(ext.at[pl.ds(4, 4)], ext.at[pl.ds(8, 4)], *near, plane_id(3, 0))
        sends.append((ext.at[pl.ds(0, 8)], near[0]))

    def apply_end(a, out, before=None):
        ext = (ext0, ext1)[a]
        four, pair, zero, one, z_four, z_pair, all_four, all_pair, all_zero, all_one, near = stage_sems[a]

        def push_z(dz, pair_of):
            b = 0 if dz < 2 else 1 if dz < 4 else 2
            push(zs.at[a, pl.ds(b * 16, 16)], zr.at[a, dz], *pair_of, column_id(dz))

        drain(r4.at[a, pl.ds(1, 15)], four[1])
        total = sb4[a, slot].astype(F32)
        for d in range(1, 16):
            total = total + r4[a, d].astype(F32)
        zs[a, 32:48] = total
        for dz in (4, 5, 7, 6):
            push_z(dz, z_four)
        drain(r24.at[a, pl.ds(1, 15)], pair[1])
        total = sb[a, slot].astype(F32)
        for d in range(1, 16):
            total = total + r24[a, d].astype(F32)
        zs[a, 0:32] = total
        for dz in (3, 2, 1):
            push_z(dz, z_pair)
        sends.append((zr.at[a, pl.ds(4, 4)], z_four[0]))
        sends.append((zr.at[a, pl.ds(1, 3)], z_pair[0]))

        drain(r0.at[a], zero[1])
        total = jnp.zeros((64, 128), F32)
        for dy in range(4):
            total = total + r0[a, dy].astype(F32)
        g0[a] = total.astype(BF16)
        for dy in (2, 1, 3):
            push(g0.at[a], cf0.at[a, y], *all_zero, plane_id(dy, 0))
        cf0[a, y] = g0[a]
        sends.append((cf0.at[a, pl.ds(0, 3)], all_zero[0]))
        drain(r1.at[a], one[1])
        total = jnp.zeros((32, 128), F32)
        for k in range(8):
            total = total + r1[a, k].astype(F32)
        g1[a] = total.astype(BF16)
        for dy in (2, 1, 3, 0):
            for dx in (1, 0):
                if dy or dx:
                    push(g1.at[a], cf1.at[a, slot1], *all_one, plane_id(dy, dx))
        cf1[a, slot1] = g1[a]
        sends.append((cf1.at[a, pl.ds(0, 7)], all_one[0]))

        drain(zr.at[a, pl.ds(4, 4)], z_four[1])
        g4[a] = (zr[a, 4] + zr[a, 5] + zr[a, 6] + zr[a, 7]).astype(BF16)
        for d in FAR:
            push(g4.at[a], cf4.at[a, slot], *all_four, plane_id(*PLANE[d]))
        sends.append((cf4.at[a, pl.ds(0, 15)], all_four[0]))
        drain(zr.at[a, pl.ds(1, 3)], z_pair[1])
        g24[a, 0:16] = zr[a, 1].astype(BF16)
        g24[a, 16:32] = (zr[a, 2] + zr[a, 3]).astype(BF16)
        for d in FAR:
            push(g24.at[a], cf24.at[a, slot], *all_pair, plane_id(*PLANE[d]))
        sends.append((cf24.at[a, pl.ds(0, 15)], all_pair[0]))
        cf4[a, slot] = g4[a]
        cf24[a, slot] = g24[a]

        if before is not None:
            before()
        drain(ext.at[pl.ds(0, 8)], near[1])
        for k in range(12):
            at = jnp.clip(cols_ref[k] - (leaf * 4 + y) * 4 + 4, 0, 11)
            xg[k * BLK : (k + 1) * BLK] = ext[at]
        out[...] = dot(bm[...], xg[...])

        drain(cf0.at[a, pl.ds(0, 3)], all_zero[1])
        for t in range(4):
            for c in range(2):
                cs[t * 32 : t * 32 + 32, c * 128 : c * 128 + 128] = cf0[a, t, c * 32 : c * 32 + 32]
        drain(cf1.at[a, pl.ds(0, 7)], all_one[1])
        for t in range(8):
            for c in range(2):
                cs[KEEP + t * 16 : KEEP + t * 16 + 16, c * 128 : c * 128 + 128] = cf1[a, t, c * 16 : c * 16 + 16]
        out[...] += dot(up[:, : 2 * KEEP], cs[: 2 * KEEP])
        drain(cf4.at[a, pl.ds(0, 15)], all_four[1])
        for t in range(16):
            g, c = t // 2, t % 2
            at = 4 * KEEP + g * 16
            cs[at : at + 16, c * 128 : c * 128 + 128] = cf4[a, t]
        out[...] += dot(up[:, 4 * KEEP :], cs[4 * KEEP :])
        drain(cf24.at[a, pl.ds(0, 15)], all_pair[1])
        for t in range(16):
            g, c = t // 2, t % 2
            for b in range(2):
                at = (b + 2) * KEEP + g * 16
                cs[at : at + 16, c * 128 : c * 128 + 128] = cf24[a, t, b * 16 : b * 16 + 16]
        out[...] += dot(up[:, 2 * KEEP : 4 * KEEP], cs[2 * KEEP : 4 * KEEP])

    b1 = s * inv_wide
    apply_start(0, b1.astype(BF16))

    def own_u():
        load_u.wait()
        hand_on(gu_hbm, ut, u_sems)
        gathered(ut, u_sems)
        hot_t = jnp.concatenate([pt[r] for r in range(4)], 1)
        up[...] = dot(hot_t, ut[...].reshape(640, 512), ((1,), (1,))).astype(BF16)

    apply_end(0, img, own_u)
    b1 = s_ref[...] * inv_wide
    p = (dg[...] - wide(shift)) * b1 + img[...]
    vec[...] = p
    apply_start(1, p.astype(BF16))
    apply_end(1, img2)
    b1 = s_ref[...] * inv_wide
    p = vec[...]
    w = dg[...] * p + img2[...]
    sum_start(1, [column_sum(v) for v in (b1 * p, p * p, b1 * w, p * w, w * w)])
    img2[...] = w
    done = len(sends)
    for what in sends:
        drain(*what)
    sum_turn(1)
    e, pp, f, g, ww = sum_end(1, 5)
    h11 = e + shift * b1b1
    delta = h11 - shift
    h21 = jnp.sqrt(jnp.maximum(pp - 2.0 * delta * e + delta * delta * b1b1, 0.0) + EPSILON)
    inv_h21 = 1.0 / h21
    h12 = (f - delta * h11) * inv_h21
    h22 = (g - delta * (pp + shift * e + f - delta * h11)) * (inv_h21 * inv_h21)
    of_w = inv_h21
    of_p = -(delta + h22) * inv_h21
    of_b = -(delta * (shift - h22) * inv_h21 + h12)
    rest = (
        of_w * of_w * ww + of_p * of_p * pp + of_b * of_b * b1b1
        + 2.0 * (of_w * of_p * g + of_w * of_b * f + of_p * of_b * e)
    )
    inv_one = 1.0 / jnp.sqrt(h11 * h11 + h21 * h21)
    cos_one = h11 * inv_one
    sin_one = h21 * inv_one
    top = cos_one * h12 + sin_one * h22
    low = cos_one * h22 - sin_one * h12
    y_two = -low * sin_one * beta / (low * low + jnp.maximum(rest, 0.0) + EPSILON)
    y_one = (cos_one * beta - top * y_two) * inv_one
    of_one = beta - y_one * h11 - y_two * h12
    of_two = -(y_one * h21 + y_two * h22) * inv_h21
    y_over = y_two * inv_h21
    rows = (
        (y_one - y_over * delta) * inv_beta,
        y_over,
        (of_one - of_two * delta - y_two * of_b) * inv_beta,
        of_two - y_two * of_p,
        -y_over,
    )
    for ref, value in zip((c0, c1, c2, c3, c4), rows):
        ref[...] = wide(value)
    for what in sends[done:]:
        drain(*what)


def combine(rhs, vec, image, c0, c1, c2, c3, c4, sol_hbm, res_hbm, sol, res, sem):
    copies = []
    for k in range(4):
        part = pl.ds(k * 128, 128)
        r, v, m = rhs[part], vec[part], image[part]
        sol[part] = c0[...] * r + c1[...] * v
        copies.append(pltpu.make_async_copy(sol.at[part], sol_hbm.at[part], sem.at[0, k]))
        copies[-1].start()
        res[part] = c2[...] * r + c3[...] * v + c4[...] * m
        copies.append(pltpu.make_async_copy(res.at[part], res_hbm.at[part], sem.at[1, k]))
        copies[-1].start()
    for copy in copies:
        copy.wait()


def local(rhs, order, diag, blocks, near_rows, near_cols, gen_u, gen_v):
    vmem, hbm = (pl.BlockSpec(memory_space=m) for m in (pltpu.VMEM, pltpu.HBM))
    scratch = [
        ((512, 256), F32),
        ((12, BLK, BLK), BF16),
        ((5, 4, 2, 16, 512), BF16),
        ((5, 4, 2, 16, 512), BF16),
        ((4, 512, BLK), BF16),
        ((512, 512), BF16),
        ((640, 512), BF16),
        ((512, 640), BF16),
        ((512, 1536), BF16),
        ((1536, 256), BF16),
        ((640, 256), BF16),
        ((512, 256), F32),
        ((512, 256), F32),
        ((2, 16, 16, 128), BF16),
        ((2, 16, 32, 128), BF16),
        ((2, 8, 32, 128), BF16),
        ((2, 4, 64, 128), BF16),
        ((2, 16, 16, 128), BF16),
        ((2, 16, 32, 128), BF16),
        ((2, 8, 32, 128), BF16),
        ((2, 4, 64, 128), BF16),
        ((2, 48, 128), F32),
        ((2, 8, 16, 128), F32),
        ((2, 16, 128), BF16),
        ((2, 32, 128), BF16),
        ((2, 32, 128), BF16),
        ((2, 64, 128), BF16),
        ((2, 16, 16, 128), BF16),
        ((2, 16, 32, 128), BF16),
        ((2, 8, 32, 128), BF16),
        ((2, 4, 64, 128), BF16),
        ((12, BLK, 256), BF16),
        ((12, BLK, 256), BF16),
        ((2, 16, 128), F32),
        ((2, 16, 16, 128), F32),
        ((2, 16, 128), F32),
        ((2, 8, 16, 128), F32),
    ]
    vec, image, *coef = pl.pallas_call(
        kernel,
        out_shape=[jax.ShapeDtypeStruct(shape, F32) for shape in (rhs.shape,) * 2 + ((1, 256),) * 5],
        in_specs=[hbm] * 8,
        out_specs=[vmem] * 7,
        scratch_shapes=[pltpu.VMEM((1, 512), jnp.int32), pltpu.VMEM((1, 512), F32)]
        + [pltpu.SMEM((12,), jnp.int32)] * 2
        + [pltpu.VMEM(*s) for s in scratch] + [pltpu.SemaphoreType.DMA((72,))],
        compiler_params=pltpu.CompilerParams(
            collective_id=0, has_side_effects=True, vmem_limit_bytes=ROOM
        ),
    )(
        *(
            pltpu.with_memory_space_constraint(value, pltpu.HBM)
            for value in (
                order.reshape(1, -1), diag.reshape(1, -1), near_rows, near_cols, rhs, blocks,
                gen_u.transpose(0, 2, 1).reshape(5, 2, 16, -1), gen_v.transpose(0, 2, 1).reshape(5, 2, 16, -1),
            )
        )
    )
    return pl.pallas_call(
        combine,
        out_shape=[jax.ShapeDtypeStruct(rhs.shape, F32)] * 2,
        in_specs=[vmem] * 8,
        out_specs=[hbm] * 2,
        scratch_shapes=[pltpu.VMEM((512, 256), F32)] * 2 + [pltpu.SemaphoreType.DMA((2, 4))],
        compiler_params=pltpu.CompilerParams(vmem_limit_bytes=LAST),
    )(rhs, vec, image, *coef)


def solution(mesh):
    in_specs = (
        P(("leaf", "rank"), "rhs"),
        P(("leaf", "rank")),
        P(("leaf", "rank")),
        P(("leaf", "rank"), None, None),
        P(("leaf", "rank")),
        P(("leaf", "rank")),
        P(None, "leaf", "rank"),
        P(None, "leaf", "rank"),
    )
    out_specs = (P(("leaf", "rank"), "rhs"), P(("leaf", "rank"), "rhs"))
    return jax.shard_map(local, mesh=mesh, in_specs=in_specs, out_specs=out_specs, check_vma=False)
```

time: 66.8 us -> 62.1 us (0.930)
  Pallas kernels: 66 us -> 61.2 us
    pallas_call x1, Pallas kernels: 64.9 us -> 60.2 us  [local(): pl.pallas_call(kernel, out_shape=[jax.ShapeDtypeStruct(shape, F32) for sh...]
where the time goes in v4:
time: 62.1 us; the launch traced here: 61.9 us
  Pallas kernels  61.2 us (99%)
  between operations  0.66 us (1%)
    pallas_call x1, Pallas kernels, local(): pl.pallas_call(kernel, out_shape=[jax.ShapeDtypeStruct(shape, F32) for sh...  60.2 us

profile of v4, /device:TPU:8, one launch (start us, length us, event | category | flops | bytes accessed | tf_op | source)
XLA Modules:
  0.0 61.9 jit_solution(16466912609386428511)
XLA Ops:
  0.6 0.0 copy-start
  0.6 60.2 %shard_map.95 = (f32[512,256]{1,0:T(8,128)S(1)}, f32[512,256]{1,0:T(8,128)S(1)}, f32[1,256]{1,0:T(1,128)S(1)}, f32[1,256]{1,0:T(1,128)S(1)}, f32[1,256]{1,0:T(1,...) custom-call(s32[1,512]{1,0:T(1,128)} %bitcast.10, f32[1,512]{1,0:T(1,128)} %bitcast.11, s32[12]{0:T(128)} %rows_hbm.1, ...), custom_call_target="tpu_custom_call" | custom-call | tf_op jit(solution)/shard_map/pallas_call | solution.py:437
  60.8 0.0 copy-done
  60.8 1.0 %shard_map.96 = (f32[512,256]{1,0:T(8,128)}, f32[512,256]{1,0:T(8,128)}) custom-call(f32[512,256]{1,0:T(8,128)S(1)} %copy-done, f32[512,256]{1,0:T(8,128)S(1)} %get-tuple-element.9.vec, f32[512,256]{1,0:T(8,128)S(1)} %get-tuple-element.10.image, f32[1,256]{1,0:T(1,128)S(1)} %get-tuple-element.11.c0, f32[1,256]{1,0:T(1,128)S(1)} %get-tuple-element.12.c1, ...), custom_call_target="tpu_custom_call" | custom-call | tf_op jit(solution)/shard_map/pallas_call | solution.py:457
Async XLA Ops:
  0.6 60.2 %copy-start = (f32[512,256]{1,0:T(8,128)S(1)}, f32[512,256]{1,0:T(8,128)}, u32[]{:S(2)}) copy-start(f32[512,256]{1,0:T(8,128)} %rhs.1) | copy-start | bytes 1572868

commit v5 on v4

--- a/solution.py
+++ b/solution.py
@@ -107,13 +107,13 @@
     def sum_start(i, values):
         rows = [v[:, c * 128 : c * 128 + 128] for v in values for c in range(2)]
         ps[i, : len(rows)] = jnp.concatenate(rows, 0)
-        part, (sent, got, _, _) = pl.ds(0, 8 + 8 * i), sum_sems[i]
+        part, (sent, got, _, _) = pl.ds(0, 4 + 6 * i), sum_sems[i]
         for d in FAR:
             push(ps.at[i, part], pr.at[i, d, part], sent, got, plane_id(*PLANE[d]))
         sends.append((pr.at[i, pl.ds(1, 15), part], sent))
 
     def sum_turn(i):
-        part, (_, got, sent, _) = pl.ds(0, 8 + 8 * i), sum_sems[i]
+        part, (_, got, sent, _) = pl.ds(0, 4 + 6 * i), sum_sems[i]
         drain(pr.at[i, pl.ds(1, 15), part], got)
         total = ps[i, part]
         for d in range(1, 16):
@@ -124,7 +124,7 @@
         sends.append((pzr.at[i, pl.ds(1, 7), part], sent))
 
     def sum_end(i, count):
-        part = pl.ds(0, 8 + 8 * i)
+        part = pl.ds(0, 4 + 6 * i)
         drain(pzr.at[i, pl.ds(1, 7), part], sum_sems[i][3])
         total = pz[i, part]
         for dz in range(1, 8):

time: 62.1 us -> 61.3 us (0.987)
  Pallas kernels: 61.2 us -> 60.4 us
    pallas_call x1, Pallas kernels: 60.2 us -> 59.4 us  [local(): pl.pallas_call(kernel, out_shape=[jax.ShapeDtypeStruct(shape, F32) for sh...]
where the time goes in v5:
time: 61.3 us; the launch traced here: 61.1 us
  Pallas kernels  60.4 us (99%)
  between operations  0.66 us (1%)
    pallas_call x1, Pallas kernels, local(): pl.pallas_call(kernel, out_shape=[jax.ShapeDtypeStruct(shape, F32) for sh...  59.4 us

profile of v5, /device:TPU:8, one launch (start us, length us, event | category | flops | bytes accessed | tf_op | source)
XLA Modules:
  0.0 61.1 jit_solution(9198395245783011019)
XLA Ops:
  0.6 0.0 copy-start
  0.6 59.4 %shard_map.95 = (f32[512,256]{1,0:T(8,128)S(1)}, f32[512,256]{1,0:T(8,128)S(1)}, f32[1,256]{1,0:T(1,128)S(1)}, f32[1,256]{1,0:T(1,128)S(1)}, f32[1,256]{1,0:T(1,...) custom-call(s32[1,512]{1,0:T(1,128)} %bitcast.10, f32[1,512]{1,0:T(1,128)} %bitcast.11, s32[12]{0:T(128)} %rows_hbm.1, ...), custom_call_target="tpu_custom_call" | custom-call | tf_op jit(solution)/shard_map/pallas_call | solution.py:437
  60.0 0.0 copy-done
  60.0 1.0 %shard_map.96 = (f32[512,256]{1,0:T(8,128)}, f32[512,256]{1,0:T(8,128)}) custom-call(f32[512,256]{1,0:T(8,128)S(1)} %copy-done, f32[512,256]{1,0:T(8,128)S(1)} %get-tuple-element.9.vec, f32[512,256]{1,0:T(8,128)S(1)} %get-tuple-element.10.image, f32[1,256]{1,0:T(1,128)S(1)} %get-tuple-element.11.c0, f32[1,256]{1,0:T(1,128)S(1)} %get-tuple-element.12.c1, ...), custom_call_target="tpu_custom_call" | custom-call | tf_op jit(solution)/shard_map/pallas_call | solution.py:457
Async XLA Ops:
  0.6 59.4 %copy-start = (f32[512,256]{1,0:T(8,128)S(1)}, f32[512,256]{1,0:T(8,128)}, u32[]{:S(2)}) copy-start(f32[512,256]{1,0:T(8,128)} %rhs.1) | copy-start | bytes 1572868
